TPU v7x, 128 devices: a whole 4x4x4 slice. The times are simulated.
128 devices in a mesh: tok: 16 (over z, x), head: 8 (over y, core).
Axes of the slice: x: 4, y: 4, z: 4, core: 2. Of those that a mesh axis runs over, the one named last changes fastest.
Arguments:
- tokens: bfloat16 [4096, 2048], P('tok', 'head'), may hold values from -6 to 6
- input_weight: bfloat16 [2048, 6144], P(None, 'head'), may hold values from -0.125 to 0.125
- output_weight: bfloat16 [2048, 2048], P('head'), may hold values from -0.5 to 0.5
- head_gain: float32 [2048], P('head'), may hold values from 0.1 to 1.9
- query_lambda_one: float32 [128], replicated, may hold values from -1.2 to 1.2
- key_lambda_one: float32 [128], replicated, may hold values from -1.2 to 1.2
- query_lambda_two: float32 [128], replicated, may hold values from -1.2 to 1.2
- key_lambda_two: float32 [128], replicated, may hold values from -1.2 to 1.2
- cache_pool: bfloat16 [1024, 8, 128, 512], P('tok', 'head'), may hold values from -160 to 160
- page_table: int32 [4096, 8], P('tok'), may hold values from 0 to 63, as said below
- cache_length: int32 [4096], P('tok'), may hold values from 1 to 1024, as said below
- cache_owner: int32 [4096, 1], P('tok'), may hold values from 0 to 15, as said below
Outputs:
- mixed: bfloat16 [4096, 2048], P('tok', 'head')
Inputs may be any that keep to these rules, and one draw needn't show every extreme that they name: `page_table`: entries index the pool pages of the request's cache owner, counted from that owner's first page. A request's first entry is one of that owner's first 8 pages and may be shared with other requests of the same owner (a common prompt); every other entry that covers a cached position belongs to that request alone; entries past the cached length are read by nobody. `cache_length`: some request has exactly 1024 cached tokens in every draw. `cache_owner`: among the 256 requests of one index of tok, at most 32 name the same owner; some owner is named by exactly 32 requests of every index.
All inputs are finite; a program needn't handle non-finite values.
Results may differ from a plain program's by a relative error of at most 0.025.
Values may be sent and summed in bfloat16 or wider, within the bound.
A program may use at most 128 MiB of HBM per device.

v0:
```python
import math

import jax
import jax.numpy as jnp
from jax import lax
from jax.sharding import PartitionSpec as P

QK = 128
VDIM = 256
PAGE = 128
KEY_PAGES = 1
GROUP = 16
CAP = 32


lambda_init = 0.8
norm_eps = 1e-05


def project_add(portion, weights):
    return jnp.dot(portion, weights, preferred_element_type=jnp.float32)


def softmax_step(softmax_state, owner_scores, values):
    running_max, total_sum, accumulated = softmax_state
    new_max = jnp.maximum(running_max, jnp.max(owner_scores, axis=(2, 3)))
    shrink = jnp.exp(running_max - new_max)
    weights = jnp.exp(owner_scores - new_max[:, :, None, None])
    total_sum = total_sum * shrink + jnp.sum(weights, axis=(2, 3))
    update = jnp.einsum(
        "ghpt,gphtv->ghv", weights.astype(jnp.bfloat16), values, preferred_element_type=jnp.float32
    )
    accumulated = accumulated * shrink[:, :, None] + update
    return (new_max, total_sum, accumulated)


def attend_group(queries, page_rows, cached, cache_pool, lambda_mix, gain_rows):
    scale_qk = 1.0 / math.sqrt(QK)
    query_one = queries[..., 0:QK]
    query_two = queries[..., QK : 2 * QK]
    key_one = queries[..., 2 * QK : 3 * QK]
    key_two = queries[..., 3 * QK : 4 * QK]
    value_new = queries[..., 4 * QK :].astype(jnp.float32)
    self_one = (
        jnp.einsum("ghd,ghd->gh", query_one, key_one, preferred_element_type=jnp.float32) * scale_qk
    )
    self_two = (
        jnp.einsum("ghd,ghd->gh", query_two, key_two, preferred_element_type=jnp.float32) * scale_qk
    )
    key_span = KEY_PAGES * PAGE
    steps_needed = (jnp.max(cached) + key_span - 1) // key_span
    within_block = jnp.arange(KEY_PAGES)[:, None] * PAGE + jnp.arange(PAGE)[None, :]
    map_one = (self_one, jnp.ones_like(self_one), value_new)
    map_two = (self_two, jnp.ones_like(self_two), value_new)

    def block_step(block_index, both_maps):
        state_one, state_two = both_maps
        page_ids = lax.dynamic_slice_in_dim(page_rows, block_index * KEY_PAGES, KEY_PAGES, 1)
        cached_keys = cache_pool[page_ids]
        values = cached_keys[..., 2 * QK :]
        positions = block_index * key_span + within_block
        is_valid = (positions[None, :, :] < cached[:, None, None])[:, None, :, :]
        score_one = (
            jnp.einsum(
                "ghd,gphtd->ghpt",
                query_one,
                cached_keys[..., 0:QK],
                preferred_element_type=jnp.float32,
            )
            * scale_qk
        )
        score_two = (
            jnp.einsum(
                "ghd,gphtd->ghpt",
                query_two,
                cached_keys[..., QK : 2 * QK],
                preferred_element_type=jnp.float32,
            )
            * scale_qk
        )
        score_one = jnp.where(is_valid, score_one, -jnp.inf)
        score_two = jnp.where(is_valid, score_two, -jnp.inf)
        return (
            softmax_step(state_one, score_one, values),
            softmax_step(state_two, score_two, values),
        )

    map_one, map_two = lax.fori_loop(0, steps_needed, block_step, (map_one, map_two))
    mixed = map_one[2] / map_one[1][..., None] - lambda_mix * (map_two[2] / map_two[1][..., None])
    scale_rms = lax.rsqrt(jnp.mean(mixed * mixed, axis=-1, keepdims=True) + norm_eps)
    normed = mixed * scale_rms * gain_rows[None] * (1.0 - lambda_init)
    return normed.reshape(normed.shape[0], -1).astype(jnp.bfloat16)


def run_owner(queries, page_rows, counts, cache_pool, lambda_mix, gain_rows):
    slot_count = queries.shape[0]
    is_live = counts > 0
    cached = jnp.maximum(counts - 1, 0)
    visit_order = jnp.argsort(-counts, stable=True)
    group_turns = (jnp.sum(is_live.astype(jnp.int32)) + GROUP - 1) // GROUP
    width_out = queries.shape[1] * VDIM
    slot_ids = jnp.arange(slot_count)

    def group_step(turn_number, results):
        chosen = lax.dynamic_slice_in_dim(visit_order, turn_number * GROUP, GROUP)
        picker = chosen[:, None] == slot_ids[None, :]
        picker_bf = picker.astype(jnp.bfloat16)
        group_queries = jnp.einsum(
            "gn,nhd->ghd", picker_bf, queries, preferred_element_type=jnp.float32
        ).astype(jnp.bfloat16)
        group_pages = jnp.sum(jnp.where(picker[:, :, None], page_rows[None, :, :], 0), axis=1)
        group_cached = jnp.sum(jnp.where(picker, cached[None, :], 0), axis=1)
        group_live = jnp.sum(jnp.where(picker, counts[None, :], 0), axis=1) > 0
        outputs = attend_group(
            group_queries, group_pages, group_cached, cache_pool, lambda_mix, gain_rows
        )
        outputs = jnp.where(group_live[:, None], outputs, jnp.zeros_like(outputs))
        placed = lax.dot_general(
            picker_bf, outputs, (((0,), (0,)), ((), ())), preferred_element_type=jnp.float32
        )
        return results + placed

    results = jnp.zeros((slot_count, width_out), jnp.float32)
    return lax.fori_loop(0, group_turns, group_step, results).astype(jnp.bfloat16)


def on_device(
    tokens,
    input_weight,
    output_weight,
    head_gain,
    query_lambda_one,
    key_lambda_one,
    query_lambda_two,
    key_lambda_two,
    cache_pool,
    page_table,
    cache_length,
    cache_owner,
):
    heads_here = input_weight.shape[1] // (4 * QK + VDIM)
    projected = project_add(lax.all_gather(tokens, "head", axis=1, tiled=True), input_weight)
    projected = projected.astype(jnp.bfloat16)
    lambda_mix = (
        jnp.exp(jnp.sum(query_lambda_one * key_lambda_one))
        - jnp.exp(jnp.sum(query_lambda_two * key_lambda_two))
        + lambda_init
    )
    gain_rows = head_gain.reshape(heads_here, VDIM)
    counts_local = cache_length + 1
    owners = cache_owner[:, 0]
    groups = lax.axis_size("tok")
    slots = groups * CAP
    one_hot = (owners[:, None] == jnp.arange(groups)[None, :]).astype(jnp.int32)
    before = jnp.cumsum(one_hot, axis=0) - one_hot
    rank_in = jnp.sum(before * one_hot, axis=1)
    slot_of = owners * CAP + rank_in
    placement = jnp.arange(slots)[:, None] == slot_of[None, :]
    placement_bf = placement.astype(jnp.bfloat16)
    send_queries = jnp.dot(placement_bf, projected, preferred_element_type=jnp.float32).astype(
        jnp.bfloat16
    )
    send_pages = jnp.sum(jnp.where(placement[:, :, None], page_table[None, :, :], 0), axis=1)
    send_counts = jnp.sum(jnp.where(placement, counts_local[None, :], 0), axis=1)
    got_queries, got_pages, got_counts = (
        lax.all_to_all(
            send_queries.reshape(groups, CAP, -1), "tok", split_axis=0, concat_axis=0, tiled=True
        ),
        lax.all_to_all(
            send_pages.reshape(groups, CAP, -1), "tok", split_axis=0, concat_axis=0, tiled=True
        ),
        lax.all_to_all(
            send_counts.reshape(groups, CAP), "tok", split_axis=0, concat_axis=0, tiled=True
        ),
    )
    results = run_owner(
        got_queries.reshape(slots, heads_here, -1),
        got_pages.reshape(slots, -1),
        got_counts.reshape(slots),
        cache_pool,
        lambda_mix,
        gain_rows,
    )
    returned = lax.all_to_all(
        results.reshape(groups, CAP, -1), "tok", split_axis=0, concat_axis=0, tiled=True
    )
    head_out = lax.dot_general(
        placement_bf,
        returned.reshape(slots, -1),
        (((0,), (0,)), ((), ())),
        preferred_element_type=jnp.float32,
    ).astype(jnp.bfloat16)
    partial_out = jnp.dot(head_out, output_weight, preferred_element_type=jnp.float32)
    mixed = lax.psum_scatter(
        partial_out.astype(jnp.bfloat16), "head", scatter_dimension=1, tiled=True
    )
    return mixed


def solution(mesh):
    placed = (
        P("tok", "head"),
        P(None, "head"),
        P("head", None),
        P("head"),
        P(),
        P(),
        P(),
        P(),
        P("tok", "head", None, None),
        P("tok", None),
        P("tok"),
        P("tok", None),
    )
    return jax.shard_map(
        on_device, mesh=mesh, in_specs=placed, out_specs=P("tok", "head"), check_vma=False
    )
```

profile of v0, /device:TPU:0, one launch (start us, length us, event | category | flops | bytes accessed | tf_op | source)
XLA Modules:
  0.0 733.9 jit_solution(7329194462999317548)
XLA Ops:
  11.9 8.0 %all-to-all-start = ((s32[16,1,32]{2,1,0:T(1,128)}), s32[16,1,32]{2,1,0:T(1,128)S(1)}, u32[]{:S(2)}, u32[]{:S(2)}) async-start(s32[16,1,32]{2,1,0:T(1,128)} %all_to_all.17), calls=%async_computation | async-start | bytes 16384 | tf_op jit(solution)/shard_map/all_to_all | solution.py:172
  20.0 9.4 %select_reduce_fusion.1 = s32[512,8]{1,0:T(8,128)S(1)} fusion(s32[256,8]{0,1:T(8,128)} %param.25, pred[512,256]{1,0:T(8,128)(4,1)S(1)} %iota_compare_fusion.3), kind=kLoop, calls=%fused_computation.81 | loop fusion | flops 2093056 | bytes 155648 | tf_op jit(solution)/shard_map/reduce_sum | solution.py:163
  30.3 7.2 all-to-all-start.2
  63.1 602.2 %while.83 = (s32[]{:T(128)}, f32[512,256]{1,0:T(8,128)}, s32[]{:T(128)}, s32[512]{0:T(512)S(1)}, s32[16,32]{1,0:T(8,128)}, /*index=5*/bf16[512,1,768]{2,0,1:T(8,...) while((s32[]{:T(128)}, f32[512,256]{1,0:T(8,128)}, ...), condition=%wide.wide.region_21.22_spmd.clone, body=%wide.wide.region_9.21_spmd.clone.sunk | while | flops 20382908 | bytes 18096756 | solution.py:124
  66.9 86.6 %while.84 = (s32[]{:T(128)}, f32[16,1]{0,1:T(1,128)S(1)}, f32[16,1]{0,1:T(1,128)S(1)}, f32[16,1,256]{2,1,0:T(1,128)S(1)}, f32[16,1]{0,1:T(1,128)S(1)}, /*index=5...) while((s32[]{:T(128)}, f32[16,1]{0,1:T(1,128)S(1)}, ...), condition=%wide.region_19.19_spmd.clone, body=%wide.region_14.18_spmd.clone.sunk | while | flops 3200278 | bytes 16007159 | solution.py:88
  66.9 5.4 gather_fusion
  77.8 5.4 gather_fusion
  99.4 5.4 gather_fusion
  110.2 5.4 gather_fusion
  121.0 5.4 gather_fusion
  131.9 5.4 gather_fusion
  142.7 5.4 gather_fusion
  159.6 10.8 %while.84 = (s32[]{:T(128)}, f32[16,1]{0,1:T(1,128)S(1)}, f32[16,1]{0,1:T(1,128)S(1)}, f32[16,1,256]{2,1,0:T(1,128)S(1)}, f32[16,1]{0,1:T(1,128)S(1)}, /*index=5...) while((s32[]{:T(128)}, f32[16,1]{0,1:T(1,128)S(1)}, ...), condition=%wide.region_19.19_spmd.clone, body=%wide.region_14.18_spmd.clone.sunk | while | flops 3200278 | bytes 16007159 | solution.py:88
  159.7 5.4 gather_fusion
  176.6 10.8 %while.84 = (s32[]{:T(128)}, f32[16,1]{0,1:T(1,128)S(1)}, f32[16,1]{0,1:T(1,128)S(1)}, f32[16,1,256]{2,1,0:T(1,128)S(1)}, f32[16,1]{0,1:T(1,128)S(1)}, /*index=5...) while((s32[]{:T(128)}, f32[16,1]{0,1:T(1,128)S(1)}, ...), condition=%wide.region_19.19_spmd.clone, body=%wide.region_14.18_spmd.clone.sunk | while | flops 3200278 | bytes 16007159 | solution.py:88
  176.6 5.4 gather_fusion
  193.6 10.8 %while.84 = (s32[]{:T(128)}, f32[16,1]{0,1:T(1,128)S(1)}, f32[16,1]{0,1:T(1,128)S(1)}, f32[16,1,256]{2,1,0:T(1,128)S(1)}, f32[16,1]{0,1:T(1,128)S(1)}, /*index=5...) while((s32[]{:T(128)}, f32[16,1]{0,1:T(1,128)S(1)}, ...), condition=%wide.region_19.19_spmd.clone, body=%wide.region_14.18_spmd.clone.sunk | while | flops 3200278 | bytes 16007159 | solution.py:88
  193.6 5.4 gather_fusion
  210.5 10.8 %while.84 = (s32[]{:T(128)}, f32[16,1]{0,1:T(1,128)S(1)}, f32[16,1]{0,1:T(1,128)S(1)}, f32[16,1,256]{2,1,0:T(1,128)S(1)}, f32[16,1]{0,1:T(1,128)S(1)}, /*index=5...) while((s32[]{:T(128)}, f32[16,1]{0,1:T(1,128)S(1)}, ...), condition=%wide.region_19.19_spmd.clone, body=%wide.region_14.18_spmd.clone.sunk | while | flops 3200278 | bytes 16007159 | solution.py:88
  210.6 5.4 gather_fusion
  227.5 10.8 %while.84 = (s32[]{:T(128)}, f32[16,1]{0,1:T(1,128)S(1)}, f32[16,1]{0,1:T(1,128)S(1)}, f32[16,1,256]{2,1,0:T(1,128)S(1)}, f32[16,1]{0,1:T(1,128)S(1)}, /*index=5...) while((s32[]{:T(128)}, f32[16,1]{0,1:T(1,128)S(1)}, ...), condition=%wide.region_19.19_spmd.clone, body=%wide.region_14.18_spmd.clone.sunk | while | flops 3200278 | bytes 16007159 | solution.py:88
  244.5 10.8 %while.84 = (s32[]{:T(128)}, f32[16,1]{0,1:T(1,128)S(1)}, f32[16,1]{0,1:T(1,128)S(1)}, f32[16,1,256]{2,1,0:T(1,128)S(1)}, f32[16,1]{0,1:T(1,128)S(1)}, /*index=5...) while((s32[]{:T(128)}, f32[16,1]{0,1:T(1,128)S(1)}, ...), condition=%wide.region_19.19_spmd.clone, body=%wide.region_14.18_spmd.clone.sunk | while | flops 3200278 | bytes 16007159 | solution.py:88
  261.5 10.8 %while.84 = (s32[]{:T(128)}, f32[16,1]{0,1:T(1,128)S(1)}, f32[16,1]{0,1:T(1,128)S(1)}, f32[16,1,256]{2,1,0:T(1,128)S(1)}, f32[16,1]{0,1:T(1,128)S(1)}, /*index=5...) while((s32[]{:T(128)}, f32[16,1]{0,1:T(1,128)S(1)}, ...), condition=%wide.region_19.19_spmd.clone, body=%wide.region_14.18_spmd.clone.sunk | while | flops 3200278 | bytes 16007159 | solution.py:88
  278.5 10.8 %while.84 = (s32[]{:T(128)}, f32[16,1]{0,1:T(1,128)S(1)}, f32[16,1]{0,1:T(1,128)S(1)}, f32[16,1,256]{2,1,0:T(1,128)S(1)}, f32[16,1]{0,1:T(1,128)S(1)}, /*index=5...) while((s32[]{:T(128)}, f32[16,1]{0,1:T(1,128)S(1)}, ...), condition=%wide.region_19.19_spmd.clone, body=%wide.region_14.18_spmd.clone.sunk | while | flops 3200278 | bytes 16007159 | solution.py:88
  295.5 10.8 %while.84 = (s32[]{:T(128)}, f32[16,1]{0,1:T(1,128)S(1)}, f32[16,1]{0,1:T(1,128)S(1)}, f32[16,1,256]{2,1,0:T(1,128)S(1)}, f32[16,1]{0,1:T(1,128)S(1)}, /*index=5...) while((s32[]{:T(128)}, f32[16,1]{0,1:T(1,128)S(1)}, ...), condition=%wide.region_19.19_spmd.clone, body=%wide.region_14.18_spmd.clone.sunk | while | flops 3200278 | bytes 16007159 | solution.py:88
  312.4 10.8 %while.84 = (s32[]{:T(128)}, f32[16,1]{0,1:T(1,128)S(1)}, f32[16,1]{0,1:T(1,128)S(1)}, f32[16,1,256]{2,1,0:T(1,128)S(1)}, f32[16,1]{0,1:T(1,128)S(1)}, /*index=5...) while((s32[]{:T(128)}, f32[16,1]{0,1:T(1,128)S(1)}, ...), condition=%wide.region_19.19_spmd.clone, body=%wide.region_14.18_spmd.clone.sunk | while | flops 3200278 | bytes 16007159 | solution.py:88
  329.4 10.8 %while.84 = (s32[]{:T(128)}, f32[16,1]{0,1:T(1,128)S(1)}, f32[16,1]{0,1:T(1,128)S(1)}, f32[16,1,256]{2,1,0:T(1,128)S(1)}, f32[16,1]{0,1:T(1,128)S(1)}, /*index=5...) while((s32[]{:T(128)}, f32[16,1]{0,1:T(1,128)S(1)}, ...), condition=%wide.region_19.19_spmd.clone, body=%wide.region_14.18_spmd.clone.sunk | while | flops 3200278 | bytes 16007159 | solution.py:88
  346.4 10.8 %while.84 = (s32[]{:T(128)}, f32[16,1]{0,1:T(1,128)S(1)}, f32[16,1]{0,1:T(1,128)S(1)}, f32[16,1,256]{2,1,0:T(1,128)S(1)}, f32[16,1]{0,1:T(1,128)S(1)}, /*index=5...) while((s32[]{:T(128)}, f32[16,1]{0,1:T(1,128)S(1)}, ...), condition=%wide.region_19.19_spmd.clone, body=%wide.region_14.18_spmd.clone.sunk | while | flops 3200278 | bytes 16007159 | solution.py:88
  363.4 10.8 %while.84 = (s32[]{:T(128)}, f32[16,1]{0,1:T(1,128)S(1)}, f32[16,1]{0,1:T(1,128)S(1)}, f32[16,1,256]{2,1,0:T(1,128)S(1)}, f32[16,1]{0,1:T(1,128)S(1)}, /*index=5...) while((s32[]{:T(128)}, f32[16,1]{0,1:T(1,128)S(1)}, ...), condition=%wide.region_19.19_spmd.clone, body=%wide.region_14.18_spmd.clone.sunk | while | flops 3200278 | bytes 16007159 | solution.py:88
  380.4 10.8 %while.84 = (s32[]{:T(128)}, f32[16,1]{0,1:T(1,128)S(1)}, f32[16,1]{0,1:T(1,128)S(1)}, f32[16,1,256]{2,1,0:T(1,128)S(1)}, f32[16,1]{0,1:T(1,128)S(1)}, /*index=5...) while((s32[]{:T(128)}, f32[16,1]{0,1:T(1,128)S(1)}, ...), condition=%wide.region_19.19_spmd.clone, body=%wide.region_14.18_spmd.clone.sunk | while | flops 3200278 | bytes 16007159 | solution.py:88
  397.4 10.8 %while.84 = (s32[]{:T(128)}, f32[16,1]{0,1:T(1,128)S(1)}, f32[16,1]{0,1:T(1,128)S(1)}, f32[16,1,256]{2,1,0:T(1,128)S(1)}, f32[16,1]{0,1:T(1,128)S(1)}, /*index=5...) while((s32[]{:T(128)}, f32[16,1]{0,1:T(1,128)S(1)}, ...), condition=%wide.region_19.19_spmd.clone, body=%wide.region_14.18_spmd.clone.sunk | while | flops 3200278 | bytes 16007159 | solution.py:88
  414.3 10.8 %while.84 = (s32[]{:T(128)}, f32[16,1]{0,1:T(1,128)S(1)}, f32[16,1]{0,1:T(1,128)S(1)}, f32[16,1,256]{2,1,0:T(1,128)S(1)}, f32[16,1]{0,1:T(1,128)S(1)}, /*index=5...) while((s32[]{:T(128)}, f32[16,1]{0,1:T(1,128)S(1)}, ...), condition=%wide.region_19.19_spmd.clone, body=%wide.region_14.18_spmd.clone.sunk | while | flops 3200278 | bytes 16007159 | solution.py:88
  431.3 10.8 %while.84 = (s32[]{:T(128)}, f32[16,1]{0,1:T(1,128)S(1)}, f32[16,1]{0,1:T(1,128)S(1)}, f32[16,1,256]{2,1,0:T(1,128)S(1)}, f32[16,1]{0,1:T(1,128)S(1)}, /*index=5...) while((s32[]{:T(128)}, f32[16,1]{0,1:T(1,128)S(1)}, ...), condition=%wide.region_19.19_spmd.clone, body=%wide.region_14.18_spmd.clone.sunk | while | flops 3200278 | bytes 16007159 | solution.py:88
  448.3 10.8 %while.84 = (s32[]{:T(128)}, f32[16,1]{0,1:T(1,128)S(1)}, f32[16,1]{0,1:T(1,128)S(1)}, f32[16,1,256]{2,1,0:T(1,128)S(1)}, f32[16,1]{0,1:T(1,128)S(1)}, /*index=5...) while((s32[]{:T(128)}, f32[16,1]{0,1:T(1,128)S(1)}, ...), condition=%wide.region_19.19_spmd.clone, body=%wide.region_14.18_spmd.clone.sunk | while | flops 3200278 | bytes 16007159 | solution.py:88
  465.3 10.8 %while.84 = (s32[]{:T(128)}, f32[16,1]{0,1:T(1,128)S(1)}, f32[16,1]{0,1:T(1,128)S(1)}, f32[16,1,256]{2,1,0:T(1,128)S(1)}, f32[16,1]{0,1:T(1,128)S(1)}, /*index=5...) while((s32[]{:T(128)}, f32[16,1]{0,1:T(1,128)S(1)}, ...), condition=%wide.region_19.19_spmd.clone, body=%wide.region_14.18_spmd.clone.sunk | while | flops 3200278 | bytes 16007159 | solution.py:88
  482.3 10.8 %while.84 = (s32[]{:T(128)}, f32[16,1]{0,1:T(1,128)S(1)}, f32[16,1]{0,1:T(1,128)S(1)}, f32[16,1,256]{2,1,0:T(1,128)S(1)}, f32[16,1]{0,1:T(1,128)S(1)}, /*index=5...) while((s32[]{:T(128)}, f32[16,1]{0,1:T(1,128)S(1)}, ...), condition=%wide.region_19.19_spmd.clone, body=%wide.region_14.18_spmd.clone.sunk | while | flops 3200278 | bytes 16007159 | solution.py:88
  499.3 10.8 %while.84 = (s32[]{:T(128)}, f32[16,1]{0,1:T(1,128)S(1)}, f32[16,1]{0,1:T(1,128)S(1)}, f32[16,1,256]{2,1,0:T(1,128)S(1)}, f32[16,1]{0,1:T(1,128)S(1)}, /*index=5...) while((s32[]{:T(128)}, f32[16,1]{0,1:T(1,128)S(1)}, ...), condition=%wide.region_19.19_spmd.clone, body=%wide.region_14.18_spmd.clone.sunk | while | flops 3200278 | bytes 16007159 | solution.py:88
  516.2 10.8 %while.84 = (s32[]{:T(128)}, f32[16,1]{0,1:T(1,128)S(1)}, f32[16,1]{0,1:T(1,128)S(1)}, f32[16,1,256]{2,1,0:T(1,128)S(1)}, f32[16,1]{0,1:T(1,128)S(1)}, /*index=5...) while((s32[]{:T(128)}, f32[16,1]{0,1:T(1,128)S(1)}, ...), condition=%wide.region_19.19_spmd.clone, body=%wide.region_14.18_spmd.clone.sunk | while | flops 3200278 | bytes 16007159 | solution.py:88
  533.2 10.8 %while.84 = (s32[]{:T(128)}, f32[16,1]{0,1:T(1,128)S(1)}, f32[16,1]{0,1:T(1,128)S(1)}, f32[16,1,256]{2,1,0:T(1,128)S(1)}, f32[16,1]{0,1:T(1,128)S(1)}, /*index=5...) while((s32[]{:T(128)}, f32[16,1]{0,1:T(1,128)S(1)}, ...), condition=%wide.region_19.19_spmd.clone, body=%wide.region_14.18_spmd.clone.sunk | while | flops 3200278 | bytes 16007159 | solution.py:88
  550.2 10.8 %while.84 = (s32[]{:T(128)}, f32[16,1]{0,1:T(1,128)S(1)}, f32[16,1]{0,1:T(1,128)S(1)}, f32[16,1,256]{2,1,0:T(1,128)S(1)}, f32[16,1]{0,1:T(1,128)S(1)}, /*index=5...) while((s32[]{:T(128)}, f32[16,1]{0,1:T(1,128)S(1)}, ...), condition=%wide.region_19.19_spmd.clone, body=%wide.region_14.18_spmd.clone.sunk | while | flops 3200278 | bytes 16007159 | solution.py:88
  567.2 10.8 %while.84 = (s32[]{:T(128)}, f32[16,1]{0,1:T(1,128)S(1)}, f32[16,1]{0,1:T(1,128)S(1)}, f32[16,1,256]{2,1,0:T(1,128)S(1)}, f32[16,1]{0,1:T(1,128)S(1)}, /*index=5...) while((s32[]{:T(128)}, f32[16,1]{0,1:T(1,128)S(1)}, ...), condition=%wide.region_19.19_spmd.clone, body=%wide.region_14.18_spmd.clone.sunk | while | flops 3200278 | bytes 16007159 | solution.py:88
  584.2 10.8 %while.84 = (s32[]{:T(128)}, f32[16,1]{0,1:T(1,128)S(1)}, f32[16,1]{0,1:T(1,128)S(1)}, f32[16,1,256]{2,1,0:T(1,128)S(1)}, f32[16,1]{0,1:T(1,128)S(1)}, /*index=5...) while((s32[]{:T(128)}, f32[16,1]{0,1:T(1,128)S(1)}, ...), condition=%wide.region_19.19_spmd.clone, body=%wide.region_14.18_spmd.clone.sunk | while | flops 3200278 | bytes 16007159 | solution.py:88
  601.2 10.8 %while.84 = (s32[]{:T(128)}, f32[16,1]{0,1:T(1,128)S(1)}, f32[16,1]{0,1:T(1,128)S(1)}, f32[16,1,256]{2,1,0:T(1,128)S(1)}, f32[16,1]{0,1:T(1,128)S(1)}, /*index=5...) while((s32[]{:T(128)}, f32[16,1]{0,1:T(1,128)S(1)}, ...), condition=%wide.region_19.19_spmd.clone, body=%wide.region_14.18_spmd.clone.sunk | while | flops 3200278 | bytes 16007159 | solution.py:88
  618.1 10.8 %while.84 = (s32[]{:T(128)}, f32[16,1]{0,1:T(1,128)S(1)}, f32[16,1]{0,1:T(1,128)S(1)}, f32[16,1,256]{2,1,0:T(1,128)S(1)}, f32[16,1]{0,1:T(1,128)S(1)}, /*index=5...) while((s32[]{:T(128)}, f32[16,1]{0,1:T(1,128)S(1)}, ...), condition=%wide.region_19.19_spmd.clone, body=%wide.region_14.18_spmd.clone.sunk | while | flops 3200278 | bytes 16007159 | solution.py:88
  635.1 10.8 %while.84 = (s32[]{:T(128)}, f32[16,1]{0,1:T(1,128)S(1)}, f32[16,1]{0,1:T(1,128)S(1)}, f32[16,1,256]{2,1,0:T(1,128)S(1)}, f32[16,1]{0,1:T(1,128)S(1)}, /*index=5...) while((s32[]{:T(128)}, f32[16,1]{0,1:T(1,128)S(1)}, ...), condition=%wide.region_19.19_spmd.clone, body=%wide.region_14.18_spmd.clone.sunk | while | flops 3200278 | bytes 16007159 | solution.py:88
  652.1 10.8 %while.84 = (s32[]{:T(128)}, f32[16,1]{0,1:T(1,128)S(1)}, f32[16,1]{0,1:T(1,128)S(1)}, f32[16,1,256]{2,1,0:T(1,128)S(1)}, f32[16,1]{0,1:T(1,128)S(1)}, /*index=5...) while((s32[]{:T(128)}, f32[16,1]{0,1:T(1,128)S(1)}, ...), condition=%wide.region_19.19_spmd.clone, body=%wide.region_14.18_spmd.clone.sunk | while | flops 3200278 | bytes 16007159 | solution.py:88
  666.4 28.0 %all_to_all.27 = bf16[16,32,256]{2,1,0:T(8,128)(2,1)S(1)} all-to-all(bf16[16,32,256]{2,1,0:T(8,128)(2,1)S(1)} %bitcast.189), channel_id=1, replica_groups=mesh['tok'=16,'head'=8] {'tok'}, dimensions={0} | all-to-all | bytes 524288 | tf_op jit(solution)/shard_map/all_to_all | solution.py:184
  697.4 29.6 %reduce-scatter.2.cloned.1.call-done = bf16[256,256]{1,0:T(8,128)(2,1)} async-done(((bf16[256,2048]{1,0:T(8,128)(2,1)}), bf16[256,256]{1,0:T(8,128)(2,1)}) %reduce-scatter.2.cloned.1.call-update) | async-done | bytes 131088 | tf_op jit(solution)/shard_map/reduce_scatter | solution.py:194
  (1394 shorter events, 550.0 us)
Async XLA Ops:
  6.5 31.0 %copy-start = (bf16[2048,768]{1,0:T(8,128)(2,1)S(1)}, bf16[2048,768]{1,0:T(8,128)(2,1)}, u32[]{:S(2)}) copy-start(bf16[2048,768]{1,0:T(8,128)(2,1)} %param.17) | copy-start | bytes 9437188
  6.5 31.0 %all-gather.2.cloned.1.call-start = ((), (), s32[]{:S(2)}) async-start(), calls=%async_computation.5 | async-start | bytes 1179648 | tf_op jit(solution)/shard_map/all_gather | solution.py:142
  11.9 18.3 %all-to-all-start = ((s32[16,1,32]{2,1,0:T(1,128)}), s32[16,1,32]{2,1,0:T(1,128)S(1)}, u32[]{:S(2)}, u32[]{:S(2)}) async-start(s32[16,1,32]{2,1,0:T(1,128)} %all_to_all.17), calls=%async_computation | async-start | bytes 16384 | tf_op jit(solution)/shard_map/all_to_all | solution.py:172
  30.3 23.3 %copy-start.3 = (s32[16,1,32]{2,1,0:T(1,128)}, s32[16,1,32]{2,1,0:T(1,128)S(1)}, u32[]{:S(2)}) copy-start(s32[16,1,32]{2,1,0:T(1,128)S(1)} %all-to-all-done) | copy-start | bytes 6148
  30.3 14.8 %all-to-all-start.2 = ((s32[16,1,256]{2,1,0:T(1,128)}), s32[16,1,256]{2,1,0:T(1,128)S(1)}, u32[]{:S(2)}, u32[]{:S(2)}) async-start(s32[16,1,256]{2,1,0:T(1,128)} %reshape.371), calls=%async_computation.2 | async-start | bytes 32768 | tf_op jit(solution)/shard_map/all_to_all | solution.py:169
  37.5 12.1 %copy-start.5 = (f32[128]{0:T(128)S(1)}, f32[128]{0:T(128)}, u32[]{:S(2)}) copy-start(f32[128]{0:T(128)} %param.22) | copy-start | bytes 1540
  37.5 12.1 %copy-start.6 = (f32[128]{0:T(128)S(1)}, f32[128]{0:T(128)}, u32[]{:S(2)}) copy-start(f32[128]{0:T(128)} %param.23) | copy-start | bytes 1540
  37.5 13.4 %copy-start.7 = (f32[128]{0:T(128)S(1)}, f32[128]{0:T(128)}, u32[]{:S(2)}) copy-start(f32[128]{0:T(128)} %param.20) | copy-start | bytes 1540
  37.5 13.4 %copy-start.8 = (f32[128]{0:T(128)S(1)}, f32[128]{0:T(128)}, u32[]{:S(2)}) copy-start(f32[128]{0:T(128)} %param.21) | copy-start | bytes 1540
  41.1 22.0 %copy-start.4 = (f32[256]{0:T(256)S(1)}, f32[256]{0:T(256)}, u32[]{:S(2)}) copy-start(f32[256]{0:T(256)} %param.19) | copy-start | bytes 3076
  45.1 17.2 %all-to-all-start.1 = ((bf16[16,32,768]{2,1,0:T(8,128)(2,1)}), bf16[16,32,768]{2,1,0:T(8,128)(2,1)}, u32[]{:S(2)}, u32[]{:S(2)}) async-start(bf16[16,32,768]{2,1,0:T(8,128)(2,1)} %bitcast.191), calls=%async_computation.1 | async-start | bytes 1572864 | tf_op jit(solution)/shard_map/all_to_all | solution.py:166
  49.5 677.5 %reduce-scatter.2.cloned.1.call-start = ((), (), s32[]{:S(2)}) async-start(), calls=%async_computation.6 | async-start | bytes 1179648 | tf_op jit(solution)/shard_map/reduce_scatter | solution.py:194
  72.4 4.9 copy-start.1
  83.2 4.9 copy-start.1
  94.0 4.9 copy-start.1
  104.8 4.9 copy-start.1
  115.6 4.9 copy-start.1
  126.5 4.9 copy-start.1
  137.3 4.9 copy-start.1
  148.1 4.9 copy-start.1
  165.1 4.9 copy-start.1
  182.1 4.9 copy-start.1
  199.0 4.9 copy-start.1
  216.0 4.9 copy-start.1
  233.0 4.9 copy-start.1
  250.0 4.9 copy-start.1
  267.0 4.9 copy-start.1
  284.0 4.9 copy-start.1
  300.9 4.9 copy-start.1
  317.9 4.9 copy-start.1
  334.9 4.9 copy-start.1
  351.9 4.9 copy-start.1
  368.9 4.9 copy-start.1
  385.9 4.9 copy-start.1
  402.8 4.9 copy-start.1
  419.8 4.9 copy-start.1
  436.8 4.9 copy-start.1
  453.8 4.9 copy-start.1
  470.8 4.9 copy-start.1
  487.8 4.9 copy-start.1
  504.7 4.9 copy-start.1
  521.7 4.9 copy-start.1
  538.7 4.9 copy-start.1
  555.7 4.9 copy-start.1
  572.7 4.9 copy-start.1
  606.6 4.9 copy-start.1
  640.6 4.9 copy-start.1
  657.6 4.9 copy-start.1
  (3 other events, 14.1 us)
Sparse Core Ops, SparseCore 0:
  9.0 25.8 all-gather.1
  697.5 29.4 reduce-scatter.1
where the time goes:
time: 748 us; the launch traced here: 734 us
  matrix products  296 us (40%)
  local copies, waits for them, and re-layouts  215 us (29%)
  other arithmetic  94.9 us (13%)
  waiting for transfers between devices  37.6 us (5%)
  blocking collectives  28 us (4%)
  loops' own time  26.4 us (4%)
  starting transfers between devices  19.7 us (3%)
  between operations  15.6 us (2%)
    gather x38, local copies, waits for them, and re-layouts, block_step(): cached_keys = cache_pool[page_ids]  206 us
    dot_general x31, matrix products, group_step(): lax.dot_general(picker_bf, outputs, (((0,), (0,)), ((), ())), preferred_e...  68.6 us
    dot_general x76, matrix products, softmax_step(): jnp.einsum('ghpt,gphtv->ghv', weights.astype(jnp.bfloat16), values, prefe...  65.3 us
    dot_general x38, matrix products, block_step(): jnp.einsum('ghd,gphtd->ghpt', query_one, cached_keys[..., 0:QK], preferre...  58.7 us
    dot_general x38, matrix products, block_step(): jnp.einsum('ghd,gphtd->ghpt', query_two, cached_keys[..., QK:2 * QK], pre...  54.1 us
    dot_general x31, matrix products, group_step(): jnp.einsum('gn,nhd->ghd', picker_bf, queries, preferred_element_type=jnp....  43.1 us
    reduce_scatter x1, waiting for transfers between devices, on_device(): lax.psum_scatter(partial_out.astype(jnp.bfloat16), 'head', scatter_dimens...  29.6 us
    all_to_all x1, blocking collectives, on_device(): lax.all_to_all(results.reshape(groups, CAP, -1), 'tok', split_axis=0, con...  28 us
  transfers between devices with their start and end apart: 5, of which 3 were waited for; matrix products, arithmetic and copies ran while one was open for 3% of the time, Pallas kernels for 0%

commit v1 on v0

v1 whole, which is shorter than its diff:
```python
import functools
import math

import jax
import jax.numpy as jnp
from jax import lax
from jax.experimental import pallas as pl
from jax.experimental.pallas import tpu as pltpu
from jax.sharding import PartitionSpec as P

QK = 128
VDIM = 256
PAGE = 128
CAP = 32
SHARED = 8
MAXP = 8
GROUP = 16
LANES = 128
ROW = 2 * QK + LANES

lambda_init = 0.8
norm_eps = 1e-05
NEG = -1e30
SCALE = math.log2(math.e) / math.sqrt(QK)
MESH = pl.DeviceIdType.MESH
F32 = jnp.float32
BF16 = jnp.bfloat16


def iota(shape, dim):
    return lax.broadcasted_iota(jnp.int32, shape, dim)


def iota_f(shape, dim):
    return iota(shape, dim).astype(F32)


def dot(a, b):
    return jnp.dot(a, b, preferred_element_type=F32)


def dot_nt(a, b):
    return lax.dot_general(a, b, (((1,), (1,)), ((), ())), preferred_element_type=F32)


def dot_tn(a, b):
    return lax.dot_general(a, b, (((0,), (0,)), ((), ())), preferred_element_type=F32)


def to_row(column, count):
    eye = iota((count, LANES), 0) == iota((count, LANES), 1)
    return jnp.sum(jnp.where(eye, column, 0.0), axis=0, keepdims=True)


def to_column(row, count):
    eye = iota((count, LANES), 0) == iota((count, LANES), 1)
    return jnp.sum(jnp.where(eye, row, 0.0), axis=1, keepdims=True)


def split3(value):
    high = value.astype(BF16).astype(F32)
    rest = value - high
    middle = rest.astype(BF16).astype(F32)
    return high, middle, rest - middle


def step_kernel(
    sizes,
    tokens,
    w_in,
    w_out,
    pool,
    gain,
    lq1,
    lk1,
    lq2,
    lk2,
    table,
    length,
    owner,
    out,
    x,
    win_v,
    wout_v,
    pool_v,
    place,
    place_t,
    meta0,
    rows_v,
    proj,
    v_new,
    sendq,
    recvq,
    sendr,
    recvr,
    match,
    full,
    part,
    first_a,
    first_b,
    page0,
    priv_a,
    priv_b,
    u_first,
    acc,
    mix_send,
    mix_recv,
    mix_own,
    ring_send,
    ring_recv,
    local_sem,
    ag_send,
    ag_recv,
    q_send,
    q_recv,
    r_send,
    r_recv,
    m_send,
    m_recv,
    g_send,
    g_recv,
):
    n_tok, n_head, count, features = sizes
    slots = n_tok * CAP
    pages = pool.shape[0]
    half = count // 2
    ny = n_head // 2
    me_t = lax.axis_index("tok")
    me_h = lax.axis_index("head")
    y, core = me_h // 2, me_h % 2
    up, down, far = (y + 1) % ny, (y + ny - 1) % ny, (y + 2) % ny

    def head_id(yy, cc):
        return yy * 2 + cc

    sib = head_id(y, 1 - core)
    h_up, h_down, h_far = head_id(up, core), head_id(down, core), head_id(far, core)

    barrier = pltpu.get_barrier_semaphore()
    for peer in (sib, h_up, h_down):
        pl.semaphore_signal(barrier, inc=1, device_id=(me_t, peer), device_id_type=MESH)
    for k in range(1, n_tok):
        pl.semaphore_signal(
            barrier, inc=1, device_id=((me_t + k) % n_tok, me_h), device_id_type=MESH
        )

    local_x = pltpu.make_async_copy(tokens, x.at[me_h], local_sem.at[0])
    local_x.start()
    load_win = pltpu.make_async_copy(w_in, win_v, local_sem.at[1])
    load_win.start()
    load_pool = pltpu.make_async_copy(pool, pool_v, local_sem.at[2])
    load_pool.start()
    load_wout = []
    for h in range(n_head):
        load = pltpu.make_async_copy(
            w_out.at[:, pl.ds(h * features, features)], wout_v.at[h], local_sem.at[3 + h]
        )
        load.start()
        load_wout.append(load)

    own = owner[...]
    named = own == iota((count, LANES), 1)
    earlier = (iota((count, count), 0) > iota((count, count), 1)).astype(F32).astype(BF16)
    before = dot(earlier, named.astype(F32).astype(BF16))
    rank = jnp.sum(jnp.where(named, before, 0.0), axis=1, keepdims=True)
    slot = own * CAP + rank.astype(jnp.int32)
    eye = iota((count, count), 0) == iota((count, count), 1)
    slot_row = jnp.sum(jnp.where(eye, slot, 0), axis=0, keepdims=True)
    place[...] = (iota((slots, count), 0) == slot_row).astype(F32).astype(BF16)
    place_t[...] = (iota((count, slots), 1) == slot).astype(F32).astype(BF16)
    length_c = jnp.sum(jnp.where(eye, length[...], 0), axis=1, keepdims=True)
    lane = iota((count, LANES), 1)
    spread = (iota((MAXP, LANES), 0) == iota((MAXP, LANES), 1)).astype(F32).astype(BF16)
    meta = dot(table[...].astype(F32).astype(BF16), spread)
    high = (length_c // 8).astype(F32)
    low = (length_c % 8).astype(F32)
    meta0[...] = meta + jnp.where(lane == 8, high, 0.0) + jnp.where(lane == 9, low, 0.0)

    pl.semaphore_wait(barrier, 3 + n_tok - 1)

    first, second = pl.ds(0, half), pl.ds(half, half)

    def share(index, source, part_rows, target):
        return pltpu.make_async_remote_copy(
            src_ref=x.at[source, part_rows],
            dst_ref=x.at[source, part_rows],
            send_sem=ag_send.at[index],
            recv_sem=ag_recv.at[index],
            device_id=(me_t, target),
            device_id_type=MESH,
        )

    local_x.wait()
    copies = {}

    def go(index, source, part_rows, target):
        copies[index] = share(index, source, part_rows, target)
        copies[index].start()

    go(0, me_h, first, h_up)
    go(2, me_h, second, h_down)
    go(1, me_h, second, h_up)
    go(3, me_h, first, h_down)
    go(6, me_h, pl.ds(0, count), sib)

    def add_chunk(source, start=False):
        rows = pl.ds(pl.multiple_of(source * features, features), features)
        update = dot(x[source], win_v[rows, 0 : 4 * QK])
        proj[...] = update if start else proj[...] + update

    load_win.wait()
    add_chunk(me_h, True)
    copies[0].wait_recv()
    go(4, h_down, first, h_up)
    go(7, h_down, first, sib)
    copies[2].wait_recv()
    go(5, h_up, second, h_down)
    go(10, h_up, second, sib)
    copies[6].wait_recv()
    add_chunk(sib)
    copies[1].wait_recv()
    go(8, h_down, second, sib)
    add_chunk(h_down)
    copies[3].wait_recv()
    go(9, h_up, first, sib)
    add_chunk(h_up)
    copies[4].wait_recv()
    go(11, h_far, first, sib)
    copies[5].wait_recv()
    go(12, h_far, second, sib)
    add_chunk(h_far)
    copies[7].wait_recv()
    copies[8].wait_recv()
    add_chunk(head_id(down, 1 - core))
    copies[9].wait_recv()
    copies[10].wait_recv()
    add_chunk(head_id(up, 1 - core))
    copies[11].wait_recv()
    copies[12].wait_recv()
    add_chunk(head_id(far, 1 - core))

    qk = proj[...].astype(BF16)
    qf = qk.astype(F32)
    self_a = jnp.sum(qf[:, 0:QK] * qf[:, 2 * QK : 3 * QK], axis=1, keepdims=True) * SCALE
    self_b = jnp.sum(qf[:, QK : 2 * QK] * qf[:, 3 * QK :], axis=1, keepdims=True) * SCALE
    meta = meta0[...]
    for index, term in enumerate(split3(self_a) + split3(self_b)):
        meta = meta + jnp.where(lane == 10 + index, term, 0.0)
    rows_v[:, 0 : 2 * QK] = qk[:, 0 : 2 * QK]
    rows_v[:, 2 * QK :] = meta.astype(BF16)
    sendq[...] = dot(place[...], rows_v[...]).astype(BF16).reshape(n_tok, CAP, ROW)
    q_copies = []
    for k in range(1, n_tok):
        target = (me_t + k) % n_tok
        copy = pltpu.make_async_remote_copy(
            src_ref=sendq.at[target],
            dst_ref=recvq.at[me_t],
            send_sem=q_send.at[k],
            recv_sem=q_recv.at[k],
            device_id=(target, me_h),
            device_id_type=MESH,
        )
        copy.start()
        q_copies.append(copy)
    recvq[me_t] = sendq[me_t]

    value = jnp.zeros((count, VDIM), F32)
    for h in range(n_head):
        value = value + dot(x[h], win_v[h * features : (h + 1) * features, 4 * QK :])
    v_new[...] = value.astype(BF16)
    lam = (
        jnp.exp(jnp.sum(lq1[...] * lk1[...], axis=1, keepdims=True))
        - jnp.exp(jnp.sum(lq2[...] * lk2[...], axis=1, keepdims=True))
        + lambda_init
    )
    load_pool.wait()
    for copy in q_copies:
        copy.wait_recv()

    blocks = slots // PAGE
    per = PAGE // CAP
    lane_f = iota_f((PAGE, LANES), 1)

    def block_rows(ref, i):
        return ref[pl.ds(i * per, per)].reshape(PAGE, ROW)

    def cut(i):
        return pl.ds(i * PAGE, PAGE)

    lengths, selfs = [], []
    for i in range(blocks):
        info = block_rows(recvq, i)[:, 2 * QK :].astype(F32)
        cached = info[:, 8:9] * 8.0 + info[:, 9:10]
        hit_any = jnp.zeros((PAGE, LANES), F32)
        hit_full = jnp.zeros((PAGE, LANES), F32)
        hit_part = jnp.zeros((PAGE, LANES), F32)
        for j in range(1, MAXP):
            left = cached - float(PAGE * j)
            number = jnp.where(left > 0.0, info[:, j : j + 1], -1.0)
            hit = number == lane_f
            whole = jnp.where(left >= float(PAGE), 1.0, 0.0)
            rest = jnp.where(left >= float(PAGE), 0.0, left)
            hit_any = jnp.where(hit, 1.0, hit_any)
            hit_full = jnp.where(hit, hit_full + whole, hit_full)
            hit_part = jnp.where(hit, hit_part + rest, hit_part)
        match[cut(i)] = hit_any.astype(BF16)
        full[cut(i)] = hit_full.astype(BF16)
        part[cut(i)] = hit_part.astype(BF16)
        page0[cut(i)] = jnp.broadcast_to(info[:, 0:1], (PAGE, LANES))
        lengths.append(cached)
        selfs.append(
            (
                info[:, 10:11] + info[:, 11:12] + info[:, 12:13],
                info[:, 13:14] + info[:, 14:15] + info[:, 15:16],
            )
        )

    queries = recvq[...].reshape(slots, ROW)[:, 0 : 2 * QK]
    ones = jnp.ones((slots, LANES), F32).astype(BF16)
    page_q = dot_tn(match[...], queries)[0:pages].astype(BF16)
    page_full = dot_tn(full[...], ones)[0:pages]
    page_part = dot_tn(part[...], ones)[0:pages]
    times = page_full + jnp.where(iota_f((pages, LANES), 1) < page_part, 1.0, 0.0)

    for g in range(0, SHARED, 2):
        keys = pool_v[g : g + 2].reshape(2 * PAGE, 2 * QK + VDIM)
        for first_ref, lo in ((first_a, 0), (first_b, QK)):
            score = dot_nt(queries[:, lo : lo + QK], keys[:, lo : lo + QK])
            chosen = jnp.where(page0[...] == float(g), score[:, 0:PAGE], score[:, PAGE:])
            if g == 0:
                first_ref[...] = chosen
            else:
                first_ref[...] = jnp.where(page0[...] >= float(g), chosen, first_ref[...])

    row = iota((GROUP, LANES), 0)

    def private_scores(g, carry):
        keys = pool_v[pl.ds(g * GROUP, GROUP)].reshape(GROUP * PAGE, 2 * QK + VDIM)
        mine = pl.ds(pl.multiple_of(g * GROUP, GROUP), GROUP)
        for ref, lo in ((priv_a, 0), (priv_b, QK)):
            score = dot_nt(acc_q[mine, lo : lo + QK], keys[:, lo : lo + QK])
            chosen = score[:, 0:PAGE]
            for i in range(1, GROUP):
                chosen = jnp.where(row == i, score[:, i * PAGE : (i + 1) * PAGE], chosen)
            ref[mine] = chosen
        return carry

    acc_q = rows_v
    rows_v[0:pages, 0 : 2 * QK] = page_q
    lax.fori_loop(0, pages // GROUP, private_scores, 0)

    priv = []
    for ref in (priv_a, priv_b):
        score = jnp.where(times > 0.0, ref[...] * SCALE, NEG)
        priv.append((score, to_row(jnp.max(score, axis=1, keepdims=True), pages)))

    tops = []
    page_top = [jnp.zeros((1, LANES), F32) for _ in range(2)]
    for i in range(blocks):
        hit = match[cut(i)].astype(F32) > 0.0
        for m, ref in enumerate((first_a, first_b)):
            score = jnp.where(lane_f < lengths[i], ref[cut(i)] * SCALE, NEG)
            ref[cut(i)] = score
            best = jnp.maximum(score, jnp.where(hit, priv[m][1], NEG))
            top = jnp.maximum(jnp.max(best, axis=1, keepdims=True), selfs[i][m])
            page_top[m] = page_top[m] + jnp.sum(
                jnp.where(hit, top, 0.0), axis=0, keepdims=True
            )
            tops.append(top)

    page_weight, page_sum = [], []
    for m in range(2):
        top = to_column(page_top[m], pages)
        weight = jnp.where(times > 0.0, jnp.exp2(priv[m][0] - top) * times, 0.0)
        page_weight.append(weight)
        page_sum.append(to_row(jnp.sum(weight, axis=1, keepdims=True), pages))

    page_coef = [jnp.zeros((1, LANES), F32) for _ in range(2)]
    for i in range(blocks):
        hit = match[cut(i)].astype(F32) > 0.0
        mixed, own_coef = None, None
        for m, ref in enumerate((first_a, first_b)):
            top = tops[2 * i + m]
            weight = jnp.exp2(ref[cut(i)] - top)
            new = jnp.exp2(selfs[i][m] - top)
            total = new + jnp.sum(
                weight + jnp.where(hit, page_sum[m], 0.0), axis=1, keepdims=True
            )
            coef = 1.0 / total if m == 0 else -lam / total
            page_coef[m] = page_coef[m] + jnp.sum(
                jnp.where(hit, coef, 0.0), axis=0, keepdims=True
            )
            mixed = weight * coef if m == 0 else mixed + weight * coef
            own_coef = new * coef if m == 0 else own_coef + new * coef
        u_first[cut(i)] = mixed.astype(BF16)
        coef_high = own_coef.astype(BF16).astype(F32)
        coefs = jnp.where(lane_f == 0.0, coef_high, 0.0) + jnp.where(
            lane_f == 1.0, own_coef - coef_high, 0.0
        )
        sendr[pl.ds(i * per, per), :, VDIM:] = coefs.astype(BF16).reshape(per, CAP, LANES)

    page_mix = page_weight[0] * to_column(page_coef[0], pages) + page_weight[1] * to_column(
        page_coef[1], pages
    )
    priv_a[...] = page_mix
    for g in range(0, SHARED, 2):
        values = pool_v[g : g + 2].reshape(2 * PAGE, 2 * QK + VDIM)[:, 2 * QK :]
        weight = u_first[...].astype(F32)
        pair = jnp.concatenate(
            [jnp.where(page0[...] == float(g + i), weight, 0.0) for i in range(2)], axis=1
        ).astype(BF16)
        update = dot(pair, values)
        acc[...] = update if g == 0 else acc[...] + update

    def private_values(g, carry):
        values = pool_v[pl.ds(g * GROUP, GROUP)].reshape(GROUP * PAGE, 2 * QK + VDIM)[:, 2 * QK :]
        mine = pl.ds(pl.multiple_of(g * GROUP, GROUP), GROUP)
        weight = priv_a[mine]
        wide = jnp.concatenate(
            [jnp.where(row == i, weight, 0.0) for i in range(GROUP)], axis=1
        ).astype(BF16)
        mix_own[0, mine] = dot(wide, values)
        return carry

    lax.fori_loop(0, pages // GROUP, private_values, 0)
    page_out = mix_own[0, 0:pages]
    page_high = page_out.astype(BF16)
    page_low = (page_out - page_high.astype(F32)).astype(BF16)
    chosen_pages = match[...][:, 0:pages]
    result = acc[...] + dot(chosen_pages, page_high) + dot(chosen_pages, page_low)
    sendr[:, :, 0:VDIM] = result.astype(BF16).reshape(n_tok, CAP, VDIM)

    r_copies = []
    for k in range(1, n_tok):
        target = (me_t + k) % n_tok
        copy = pltpu.make_async_remote_copy(
            src_ref=sendr.at[target],
            dst_ref=recvr.at[me_t],
            send_sem=r_send.at[k],
            recv_sem=r_recv.at[k],
            device_id=(target, me_h),
            device_id_type=MESH,
        )
        copy.start()
        r_copies.append(copy)
    recvr[me_t] = sendr[me_t]
    for load in load_wout:
        load.wait()
    for copy in r_copies:
        copy.wait_recv()

    got = dot(place_t[...], recvr[...].reshape(slots, ROW))
    coef = got[:, VDIM : VDIM + 1] + got[:, VDIM + 1 : VDIM + 2]
    mixed = got[:, 0:VDIM] + coef * v_new[...].astype(F32)
    scale = lax.rsqrt(jnp.mean(mixed * mixed, axis=1, keepdims=True) + norm_eps)
    head_out = (mixed * scale * gain[...] * (1.0 - lambda_init)).astype(BF16)

    order = (far, up, down, y)
    mixes = []
    for k, yy in enumerate(order):
        mix_send[k] = dot(head_out, wout_v[head_id(yy, 1 - core)]).astype(BF16)
        copy = pltpu.make_async_remote_copy(
            src_ref=mix_send.at[k],
            dst_ref=mix_recv.at[k],
            send_sem=m_send.at[k],
            recv_sem=m_recv.at[k],
            device_id=(me_t, sib),
            device_id_type=MESH,
        )
        copy.start()
        mixes.append(copy)
    for k, yy in enumerate(order):
        mix_own[k] = dot(head_out, wout_v[head_id(yy, core)])

    rings = {}

    def ring(index, value, target):
        ring_send[index] = value.astype(BF16)
        rings[index] = pltpu.make_async_remote_copy(
            src_ref=ring_send.at[index],
            dst_ref=ring_recv.at[index],
            send_sem=g_send.at[index],
            recv_sem=g_recv.at[index],
            device_id=(me_t, target),
            device_id_type=MESH,
        )
        rings[index].start()

    def chip_sum(k):
        mixes[k].wait_recv()
        return mix_own[k] + mix_recv[k].astype(F32)

    total = chip_sum(0)
    ring(0, total[0:half], h_up)
    ring(1, total[half:], h_down)
    to_up = chip_sum(1)
    ring(2, to_up[half:], h_up)
    to_down = chip_sum(2)
    ring(3, to_down[0:half], h_down)
    rings[0].wait_recv()
    ring(4, to_up[0:half] + ring_recv[0].astype(F32), h_up)
    rings[1].wait_recv()
    ring(5, to_down[half:] + ring_recv[1].astype(F32), h_down)
    total = chip_sum(3)
    for index in (2, 3, 4, 5):
        rings[index].wait_recv()
    out[0:half] = (
        total[0:half] + ring_recv[4].astype(F32) + ring_recv[3].astype(F32)
    ).astype(BF16)
    out[half:] = (total[half:] + ring_recv[2].astype(F32) + ring_recv[5].astype(F32)).astype(BF16)

    for index in range(13):
        copies[index].wait_send()
    for copy in q_copies + r_copies + mixes:
        copy.wait_send()
    for index in range(6):
        rings[index].wait_send()


def on_device(sizes, tokens, w_in, w_out, gain, lq1, lk1, lq2, lk2, pool, table, length, owner):
    n_tok, n_head, count, features = sizes
    slots = n_tok * CAP
    pages = pool.shape[0]
    half = count // 2
    vmem = pl.BlockSpec(memory_space=pltpu.VMEM)
    hbm = pl.BlockSpec(memory_space=pl.ANY)
    dma = pltpu.SemaphoreType.DMA
    return pl.pallas_call(
        functools.partial(step_kernel, sizes),
        out_shape=jax.ShapeDtypeStruct((count, features), BF16),
        in_specs=[hbm] * 4 + [vmem] * 8,
        out_specs=vmem,
        scratch_shapes=[
            pltpu.VMEM((n_head, count, features), BF16),
            pltpu.VMEM(w_in.shape, BF16),
            pltpu.VMEM((n_head, VDIM, features), BF16),
            pltpu.VMEM((pages, PAGE, 2 * QK + VDIM), BF16),
            pltpu.VMEM((slots, count), BF16),
            pltpu.VMEM((count, slots), BF16),
            pltpu.VMEM((count, LANES), F32),
            pltpu.VMEM((count, ROW), BF16),
            pltpu.VMEM((count, 4 * QK), F32),
            pltpu.VMEM((count, VDIM), BF16),
            pltpu.VMEM((n_tok, CAP, ROW), BF16),
            pltpu.VMEM((n_tok, CAP, ROW), BF16),
            pltpu.VMEM((n_tok, CAP, ROW), BF16),
            pltpu.VMEM((n_tok, CAP, ROW), BF16),
            pltpu.VMEM((slots, LANES), BF16),
            pltpu.VMEM((slots, LANES), BF16),
            pltpu.VMEM((slots, LANES), BF16),
            pltpu.VMEM((slots, PAGE), F32),
            pltpu.VMEM((slots, PAGE), F32),
            pltpu.VMEM((slots, LANES), F32),
            pltpu.VMEM((pages, PAGE), F32),
            pltpu.VMEM((pages, PAGE), F32),
            pltpu.VMEM((slots, PAGE), BF16),
            pltpu.VMEM((slots, VDIM), F32),
            pltpu.VMEM((4, count, features), BF16),
            pltpu.VMEM((4, count, features), BF16),
            pltpu.VMEM((4, count, features), F32),
            pltpu.VMEM((6, half, features), BF16),
            pltpu.VMEM((6, half, features), BF16),
            dma((3 + n_head,)),
            dma((13,)),
            dma((13,)),
            dma((n_tok,)),
            dma((n_tok,)),
            dma((n_tok,)),
            dma((n_tok,)),
            dma((4,)),
            dma((4,)),
            dma((6,)),
            dma((6,)),
        ],
        compiler_params=pltpu.CompilerParams(
            collective_id=0, has_side_effects=True, vmem_limit_bytes=60 * 1024 * 1024
        ),
        name="decode_step",
    )(
        tokens,
        w_in,
        w_out,
        pool.reshape(pages, PAGE, 2 * QK + VDIM),
        gain.reshape(1, VDIM),
        lq1.reshape(1, QK),
        lk1.reshape(1, QK),
        lq2.reshape(1, QK),
        lk2.reshape(1, QK),
        table,
        length.reshape(1, count),
        owner,
    )


def solution(mesh):
    n_tok, n_head = mesh.shape["tok"], mesh.shape["head"]

    def run(
        tokens,
        input_weight,
        output_weight,
        head_gain,
        query_lambda_one,
        key_lambda_one,
        query_lambda_two,
        key_lambda_two,
        cache_pool,
        page_table,
        cache_length,
        cache_owner,
    ):
        sizes = (n_tok, n_head, tokens.shape[0] // n_tok, tokens.shape[1] // n_head)
        placed = (
            P("tok", "head"),
            P(None, "head"),
            P("head", None),
            P("head"),
            P(),
            P(),
            P(),
            P(),
            P("tok", "head", None, None),
            P("tok", None),
            P("tok"),
            P("tok", None),
        )
        return jax.shard_map(
            functools.partial(on_device, sizes),
            mesh=mesh,
            in_specs=placed,
            out_specs=P("tok", "head"),
            check_vma=False,
        )(
            tokens,
            input_weight,
            output_weight,
            head_gain,
            query_lambda_one,
            key_lambda_one,
            query_lambda_two,
            key_lambda_two,
            cache_pool,
            page_table,
            cache_length,
            cache_owner,
        )

    return run
```

time: 748 us -> 57.5 us (0.08)
  the two profiles are of different devices: /device:TPU:0 before, /device:TPU:1 now
where the time goes in v1:
time: 57.5 us; the launch traced here: 57.3 us
  Pallas kernels  52.8 us (92%)
  local copies, waits for them, and re-layouts  4.51 us (8%)
    pallas_call x1, Pallas kernels, on_device(): pl.pallas_call(functools.partial(step_kernel, sizes), out_shape=jax.Shape...  52.8 us
    unnamed x3, local copies, waits for them, and re-layouts  4.51 us

profile of v1, /device:TPU:1, one launch (start us, length us, event | category | flops | bytes accessed | tf_op | source)
XLA Modules:
  0.0 57.3 jit_solution(14935275388874507520)
XLA Ops:
  0.0 1.5 %copy.13.table = s32[256,8]{1,0:T(8,128)} copy(s32[256,8]{0,1:T(8,128)} %param.21) | data formatting | bytes 16384 | tf_op args[9]
  1.5 1.5 %copy.14.owner = s32[256,1]{1,0:T(8,128)} copy(s32[256,1]{0,1:T(1,128)} %param.23) | data formatting | bytes 2048 | tf_op args[11]
  2.9 52.8 %decode_step.1 = bf16[256,256]{1,0:T(8,128)(2,1)} custom-call(bf16[256,256]{1,0:T(8,128)(2,1)} %tokens.1, bf16[2048,768]{1,0:T(8,128)(2,1)} %w_in.1, bf16[256,2048]{1,0:T(8,128)(2,1)} %w_out.1, bf16[64,128,512]{2,1,0:T(8,128)(2,1)} %bitcast.7, f32[1,256]{1,0:T(1,128)} %bitcast.8, f32[1,128]{1,0:T(1,128)} %bitcast.10, f32[1,128]{1,0:T(1,128)} %bitcast.11, ...), custom_call_target="tpu_custom_call" | custom-call | tf_op jit(solution)/shard_map/decode_step/pallas_call | solution.py:528
  55.8 1.6 %copy.16 = bf16[256,256]{1,0:T(8,128)(2,1)} copy(bf16[256,256]{1,0:T(8,128)(2,1)} %decode_step.1) | data formatting | bytes 262144

commit v2 on v1

v2 whole, which is shorter than its diff:
```python
import functools
import math

import jax
import jax.numpy as jnp
from jax import lax
from jax.experimental import pallas as pl
from jax.experimental.pallas import tpu as pltpu
from jax.sharding import PartitionSpec as P

QK = 128
VDIM = 256
PAGE = 128
CAP = 32
SHARED = 8
MAXP = 8
GROUP = 16
LANES = 128
FIELDS = 16
TILE = 8
PER = LANES // CAP
WIDE = 2 * QK + VDIM

lambda_init = 0.8
norm_eps = 1e-05
NEG = -1e30
SCALE = math.log2(math.e) / math.sqrt(QK)
MESH = pl.DeviceIdType.MESH
F32 = jnp.float32
BF16 = jnp.bfloat16


def iota(shape, dim):
    return lax.broadcasted_iota(jnp.int32, shape, dim)


def one_hot(condition):
    return condition.astype(F32).astype(BF16)


def dot(a, b):
    return jnp.dot(a, b, preferred_element_type=F32)


def dot_nt(a, b):
    return lax.dot_general(a, b, (((1,), (1,)), ((), ())), preferred_element_type=F32)


def split(value, terms):
    parts = []
    for _ in range(terms - 1):
        high = value.astype(BF16).astype(F32)
        parts.append(high)
        value = value - high
    return parts + [value]


def stack_rows(rows, height):
    row = iota((height, rows[0].shape[1]), 0)
    stacked = jnp.where(row == 0, rows[0], 0.0)
    for index in range(1, len(rows)):
        stacked = jnp.where(row == index, rows[index], stacked)
    return stacked


def step_kernel(
    sizes,
    tokens,
    w_in,
    w_out,
    pool,
    gain,
    lq1,
    lk1,
    lq2,
    lk2,
    table,
    length,
    owner,
    out,
    x,
    win_v,
    wcol_v,
    pool_v,
    heads,
    place,
    place_t,
    turn,
    proj,
    v_new,
    send_m,
    recv_m,
    send_q,
    recv_q,
    send_s,
    recv_s,
    send_r,
    recv_r,
    send_c,
    recv_c,
    info,
    match,
    match_t,
    times,
    page0,
    first_a,
    first_b,
    page_q,
    priv_a,
    priv_b,
    page_out,
    wide,
    local_sem,
    x_send,
    x_recv,
    m_send,
    m_recv,
    q_send,
    q_recv,
    s_send,
    s_recv,
    w_send,
    w_recv,
    c_send,
    c_recv,
    r_send,
    r_recv,
    h_send,
    h_recv,
):
    n_tok, n_head, count, features = sizes
    slots = n_tok * CAP
    blocks = slots // LANES
    pages = pool.shape[0]
    ny = n_head // 2
    nx = 4
    nz = n_tok // nx
    me_t = lax.axis_index("tok")
    me_h = lax.axis_index("head")
    y, core = me_h // 2, me_h % 2
    z_at, x_at = me_t // nx, me_t % nx
    up, down, far = (y + 1) % ny, (y + ny - 1) % ny, (y + 2) % ny
    sib = y * 2 + 1 - core
    near = (up * 2 + core, down * 2 + core, far * 2 + core)
    across = (up * 2 + 1 - core, down * 2 + 1 - core, far * 2 + 1 - core)

    offsets = [(dz, dx) for dz in range(nz) for dx in range(nx) if dz + dx > 0]
    offsets.sort(key=lambda o: -(min(o[0], nz - o[0]) + min(o[1], nx - o[1])))
    peers = [((z_at + dz) % nz) * nx + (x_at + dx) % nx for dz, dx in offsets]

    barrier = pltpu.get_barrier_semaphore()
    for peer in (sib,) + near + across:
        pl.semaphore_signal(barrier, inc=1, device_id=(me_t, peer), device_id_type=MESH)
    for peer in peers:
        pl.semaphore_signal(barrier, inc=1, device_id=(peer, me_h), device_id_type=MESH)

    sent = []

    def remote(source, target, send_sem, recv_sem, device):
        copy = pltpu.make_async_remote_copy(
            src_ref=source,
            dst_ref=target,
            send_sem=send_sem,
            recv_sem=recv_sem,
            device_id=device,
            device_id_type=MESH,
        )
        copy.start()
        sent.append(copy)
        return copy

    def exchange(source, target, send_sem, recv_sem):
        copies = [
            remote(source.at[p], target.at[me_t], send_sem.at[k], recv_sem.at[k], (p, me_h))
            for k, p in enumerate(peers)
        ]
        target[me_t] = source[me_t]
        return copies

    local_x = pltpu.make_async_copy(tokens, x.at[me_h], local_sem.at[0])
    local_x.start()
    load_win = pltpu.make_async_copy(w_in, win_v, local_sem.at[1])
    load_win.start()

    own = owner[...]
    named = own == iota((n_tok, count), 0)
    earlier = one_hot(iota((count, count), 0) < iota((count, count), 1))
    before = dot(one_hot(named), earlier)
    rank = jnp.sum(jnp.where(named, before, 0.0), axis=0, keepdims=True)
    slot = own * CAP + rank.astype(jnp.int32)
    eye = iota((count, count), 0) == iota((count, count), 1)
    slot_c = jnp.sum(jnp.where(eye, slot, 0), axis=1, keepdims=True)
    place[...] = one_hot(iota((slots, count), 0) == slot)
    place_t[...] = one_hot(iota((count, slots), 1) == slot_c)
    shift = (me_t % PER) * CAP
    for b in range(PER):
        source_lane = iota((LANES, LANES), 0)
        moved = source_lane - b * CAP + shift == iota((LANES, LANES), 1)
        turn[b] = one_hot(moved & (source_lane // CAP == b))

    def tiles(rows, height, target):
        groups = jnp.concatenate(
            [rows[:, g * LANES : (g + 1) * LANES] for g in range(blocks)], axis=0
        ).astype(BF16)
        for b in range(PER):
            moved = dot(groups, turn[b]).astype(BF16)
            for g in range(blocks):
                target[g * PER + b] = moved[g * height : (g + 1) * height]

    def gather_tiles(source, g):
        total = source[g * PER].astype(F32)
        for b in range(1, PER):
            total = total + source[g * PER + b].astype(F32)
        return total

    lengths = length[...]
    ends = stack_rows([(lengths // 8).astype(F32), (lengths % 8).astype(F32)], 8)
    fields = jnp.concatenate([table[...].astype(F32), ends], axis=0).astype(BF16)
    tiles(dot(fields, place_t[...]), FIELDS, send_m)

    pl.semaphore_wait(barrier, 1 + 2 * len(near) + len(peers))

    def gather_start(buffer, send_sem, recv_sem):
        def share(index, source, target):
            return remote(
                buffer.at[source],
                buffer.at[source],
                send_sem.at[index],
                recv_sem.at[index],
                (me_t, target),
            )

        direct = [share(k, me_h, target) for k, target in enumerate(near)]
        return share, direct, share(3, me_h, sib)

    def gather_rest(started, add):
        share, direct, twin = started
        add(me_h)
        twin.wait_recv()
        add(sib)
        passed = []
        for k, turned in enumerate((1, 0, 2)):
            direct[k].wait_recv()
            passed.append(share(4 + k, near[turned], sib))
            add(near[turned])
            if k > 0:
                passed[k - 1].wait_recv()
                add(across[(1, 0, 2)[k - 1]])
        passed[2].wait_recv()
        add(across[2])

    local_x.wait()
    started = gather_start(x, x_send, x_recv)
    m_copies = exchange(send_m, recv_m, m_send, m_recv)
    load_win.wait()
    load_pool = pltpu.make_async_copy(pool, pool_v, local_sem.at[2])
    load_pool.start()

    def add_proj(source):
        rows = pl.ds(pl.multiple_of(source * features, features), features)
        update = dot(x[source], win_v[rows, 0 : 4 * QK])
        proj[...] = proj[...] + update

    proj[...] = jnp.zeros(proj.shape, F32)
    gather_rest(started, add_proj)

    qk = proj[...].astype(BF16)
    send_q[...] = dot(place[...], qk[:, 0 : 2 * QK]).astype(BF16).reshape(n_tok, CAP, 2 * QK)
    q_copies = exchange(send_q, recv_q, q_send, q_recv)
    qf = qk.astype(F32)
    ones = jnp.ones((8, QK), F32).astype(BF16)
    terms = []
    for m in range(2):
        product = qf[:, m * QK : (m + 1) * QK] * qf[:, (m + 2) * QK : (m + 3) * QK]
        high, low = split(product, 2)
        total = dot_nt(ones, high.astype(BF16)) + dot_nt(ones, low.astype(BF16))
        terms += split(total[0:1] * SCALE, 3)
    tiles(dot(stack_rows(terms, TILE).astype(BF16), place_t[...]), TILE, send_s)
    s_copies = exchange(send_s, recv_s, s_send, s_recv)

    def columns(h):
        return w_out.at[:, pl.ds(pl.multiple_of(h * features, features), features)]

    own_w = pltpu.make_async_copy(columns(me_h), wcol_v.at[me_h], local_sem.at[3])
    own_w.start()
    w_copies = [
        remote(columns(h), wcol_v.at[me_h], w_send.at[k], w_recv.at[k], (me_t, h))
        for k, h in enumerate(near + across + (sib,))
    ]

    value = jnp.zeros((count, VDIM), F32)
    for h in range(n_head):
        value = value + dot(x[h], win_v[h * features : (h + 1) * features, 4 * QK :])
    v_new[...] = value.astype(BF16)
    lam = (
        jnp.exp(jnp.sum(lq1[...] * lk1[...], axis=1, keepdims=True))
        - jnp.exp(jnp.sum(lq2[...] * lk2[...], axis=1, keepdims=True))
        + lambda_init
    )

    for copy in m_copies:
        copy.wait_recv()
    whole = jnp.zeros((pages, LANES), F32)
    rest = jnp.zeros((pages, LANES), F32)
    page = iota((pages, LANES), 0).astype(F32)
    for g in range(blocks):
        cut = slice(g * LANES, (g + 1) * LANES)
        got = gather_tiles(recv_m, g)
        cached = got[8:9] * 8.0 + got[9:10]
        info[0:1, cut] = got[0:1]
        info[1:2, cut] = cached
        hit_any = jnp.zeros((pages, LANES), F32)
        for j in range(1, MAXP):
            left = cached - float(PAGE * j)
            number = jnp.where(left > 0.0, got[j : j + 1], -1.0)
            hit = number == page
            hit_any = jnp.where(hit, 1.0, hit_any)
            whole = whole + jnp.where(hit, jnp.where(left >= float(PAGE), 1.0, 0.0), 0.0)
            rest = rest + jnp.where(hit, jnp.where(left >= float(PAGE), 0.0, left), 0.0)
        match[:, cut] = hit_any.astype(BF16)
        match_t[cut] = jnp.transpose(jnp.concatenate([hit_any, hit_any], axis=0)).astype(BF16)
        chosen = jnp.transpose(jnp.broadcast_to(got[0:1], (LANES, LANES)))
        for p in range(SHARED):
            page0[p, cut] = one_hot(chosen == float(p))
    whole = jnp.sum(whole, axis=1, keepdims=True)
    rest = jnp.sum(rest, axis=1, keepdims=True)
    position = iota((pages, PAGE), 1).astype(F32)
    times[...] = whole + jnp.where(position < rest, 1.0, 0.0)
    load_pool.wait()
    for copy in q_copies:
        copy.wait_recv()

    queries = recv_q[...].reshape(slots, 2 * QK)
    page_q[...] = dot(match[...], queries).astype(BF16)
    half = slots // 2
    for h in range(2):
        cut = slice(h * half, (h + 1) * half)
        at = info[0:1, cut]
        for ref, lo in ((first_a, 0), (first_b, QK)):
            kept = None
            for p in range(0, SHARED, 2):
                keys = pool_v[p : p + 2].reshape(2 * PAGE, WIDE)[:, lo : lo + QK]
                score = dot_nt(keys, queries[cut, lo : lo + QK])
                chosen = jnp.where(at == float(p), score[0:PAGE], score[PAGE:])
                kept = chosen if p == 0 else jnp.where(at >= float(p), chosen, kept)
            ref[:, cut] = kept

    row = iota((GROUP, LANES), 0)

    def private_scores(g, carry):
        mine = pl.ds(pl.multiple_of(g * GROUP, GROUP), GROUP)
        keys = pool_v[mine].reshape(GROUP * PAGE, WIDE)
        for ref, lo in ((priv_a, 0), (priv_b, QK)):
            score = dot_nt(page_q[mine, lo : lo + QK], keys[:, lo : lo + QK])
            chosen = score[:, 0:PAGE]
            for i in range(1, GROUP):
                chosen = jnp.where(row == i, score[:, i * PAGE : (i + 1) * PAGE], chosen)
            ref[mine] = chosen
        return carry

    lax.fori_loop(0, pages // GROUP, private_scores, 0)

    for copy in s_copies:
        copy.wait_recv()
    page_best = []
    for ref in (priv_a, priv_b):
        score = jnp.where(times[...] > 0.0, ref[...] * SCALE, NEG)
        ref[...] = score
        page_best.append(jnp.max(score, axis=1, keepdims=True))
    tops, selfs = [], []
    page_top = [jnp.zeros((pages, LANES), F32) for _ in range(2)]
    depth = iota((PAGE, LANES), 0).astype(F32)
    for g in range(blocks):
        cut = slice(g * LANES, (g + 1) * LANES)
        hit = match[:, cut].astype(F32) > 0.0
        got = gather_tiles(recv_s, g)
        valid = depth < info[1:2, cut]
        for m, ref in enumerate((first_a, first_b)):
            score = jnp.where(valid, ref[:, cut] * SCALE, NEG)
            ref[:, cut] = score
            mine = got[3 * m : 3 * m + 1] + got[3 * m + 1 : 3 * m + 2] + got[3 * m + 2 : 3 * m + 3]
            best = jnp.max(jnp.where(hit, page_best[m], NEG), axis=0, keepdims=True)
            top = jnp.maximum(jnp.maximum(jnp.max(score, axis=0, keepdims=True), best), mine)
            page_top[m] = page_top[m] + jnp.where(hit, top, 0.0)
            tops.append(top)
            selfs.append(mine)

    page_sum = []
    for m, ref in enumerate((priv_a, priv_b)):
        top = jnp.sum(page_top[m], axis=1, keepdims=True)
        weight = jnp.where(times[...] > 0.0, jnp.exp2(ref[...] - top) * times[...], 0.0)
        ref[...] = weight
        page_sum.append(jnp.sum(weight, axis=1, keepdims=True))
    page_coef = [jnp.zeros((pages, LANES), F32) for _ in range(2)]
    own_rows = []
    for g in range(blocks):
        cut = slice(g * LANES, (g + 1) * LANES)
        hit = match[:, cut].astype(F32) > 0.0
        mixed, own_coef = None, None
        for m, ref in enumerate((first_a, first_b)):
            top = tops[2 * g + m]
            weight = jnp.exp2(ref[:, cut] - top)
            new = jnp.exp2(selfs[2 * g + m] - top)
            total = (
                new
                + jnp.sum(weight, axis=0, keepdims=True)
                + jnp.sum(jnp.where(hit, page_sum[m], 0.0), axis=0, keepdims=True)
            )
            coef = 1.0 / total if m == 0 else -lam / total
            page_coef[m] = page_coef[m] + jnp.where(hit, coef, 0.0)
            mixed = weight * coef if m == 0 else mixed + weight * coef
            own_coef = new * coef if m == 0 else own_coef + new * coef
        mixed = jnp.transpose(mixed).astype(BF16)
        for p in range(SHARED):
            wide[cut, p * PAGE : (p + 1) * PAGE] = mixed * page0[p, cut]
        own_rows.append(stack_rows(split(own_coef, 2), TILE))
    tiles(jnp.concatenate(own_rows, axis=1), TILE, send_c)
    c_copies = exchange(send_c, recv_c, c_send, c_recv)

    priv_a[...] = priv_a[...] * jnp.sum(page_coef[0], axis=1, keepdims=True) + priv_b[
        ...
    ] * jnp.sum(page_coef[1], axis=1, keepdims=True)

    def private_values(g, carry):
        mine = pl.ds(pl.multiple_of(g * GROUP, GROUP), GROUP)
        values = pool_v[mine].reshape(GROUP * PAGE, WIDE)[:, 2 * QK :]
        weight = priv_a[mine]
        spread = jnp.concatenate(
            [jnp.where(row == i, weight, 0.0) for i in range(GROUP)], axis=1
        ).astype(BF16)
        page_out[mine] = dot(spread, values)
        return carry

    lax.fori_loop(0, pages // GROUP, private_values, 0)
    high, low = split(page_out[...], 2)
    pair = jnp.concatenate([high, low], axis=0).astype(BF16)
    values = pool_v[0:SHARED].reshape(SHARED * PAGE, WIDE)[:, 2 * QK :]
    result = dot(wide[...], values) + dot(match_t[...], pair)
    send_r[...] = result.astype(BF16).reshape(n_tok, CAP, VDIM)

    r_copies = exchange(send_r, recv_r, r_send, r_recv)
    own_w.wait()
    for copy in c_copies:
        copy.wait_recv()
    rows = jnp.concatenate([gather_tiles(recv_c, g) for g in range(blocks)], axis=1)
    coefs = dot_nt(place_t[...], rows.astype(BF16))
    addend = (coefs[:, 0:1] + coefs[:, 1:2]) * v_new[...].astype(F32)
    for copy in r_copies:
        copy.wait_recv()
    mixed = dot(place_t[...], recv_r[...].reshape(slots, VDIM)) + addend
    scale = lax.rsqrt(jnp.mean(mixed * mixed, axis=1, keepdims=True) + norm_eps)
    heads[me_h] = (mixed * scale * gain[...] * (1.0 - lambda_init)).astype(BF16)

    started = gather_start(heads, h_send, h_recv)
    for copy in w_copies:
        copy.wait_recv()
    mix = proj.at[:, 0:features]
    mix[...] = jnp.zeros(mix.shape, F32)

    def add_out(source):
        mix[...] = mix[...] + dot(heads[source], wcol_v[source])

    gather_rest(started, add_out)
    out[...] = mix[...].astype(BF16)
    for copy in sent:
        copy.wait_send()


def on_device(sizes, tokens, w_in, w_out, gain, lq1, lk1, lq2, lk2, pool, table, length, owner):
    n_tok, n_head, count, features = sizes
    slots = n_tok * CAP
    pages = pool.shape[0]
    vmem = pl.BlockSpec(memory_space=pltpu.VMEM)
    hbm = pl.BlockSpec(memory_space=pl.ANY)
    dma = pltpu.SemaphoreType.DMA
    return pl.pallas_call(
        functools.partial(step_kernel, sizes),
        out_shape=jax.ShapeDtypeStruct((count, features), BF16),
        in_specs=[hbm] * 4 + [vmem] * 8,
        out_specs=vmem,
        scratch_shapes=[
            pltpu.VMEM((n_head, count, features), BF16),
            pltpu.VMEM(w_in.shape, BF16),
            pltpu.VMEM((n_head, VDIM, features), BF16),
            pltpu.VMEM((pages, PAGE, WIDE), BF16),
            pltpu.VMEM((n_head, count, VDIM), BF16),
            pltpu.VMEM((slots, count), BF16),
            pltpu.VMEM((count, slots), BF16),
            pltpu.VMEM((PER, LANES, LANES), BF16),
            pltpu.VMEM((count, 4 * QK), F32),
            pltpu.VMEM((count, VDIM), BF16),
            pltpu.VMEM((n_tok, FIELDS, LANES), BF16),
            pltpu.VMEM((n_tok, FIELDS, LANES), BF16),
            pltpu.VMEM((n_tok, CAP, 2 * QK), BF16),
            pltpu.VMEM((n_tok, CAP, 2 * QK), BF16),
            pltpu.VMEM((n_tok, TILE, LANES), BF16),
            pltpu.VMEM((n_tok, TILE, LANES), BF16),
            pltpu.VMEM((n_tok, CAP, VDIM), BF16),
            pltpu.VMEM((n_tok, CAP, VDIM), BF16),
            pltpu.VMEM((n_tok, TILE, LANES), BF16),
            pltpu.VMEM((n_tok, TILE, LANES), BF16),
            pltpu.VMEM((8, slots), F32),
            pltpu.VMEM((pages, slots), BF16),
            pltpu.VMEM((slots, 2 * pages), BF16),
            pltpu.VMEM((pages, PAGE), F32),
            pltpu.VMEM((SHARED, slots, PAGE), BF16),
            pltpu.VMEM((PAGE, slots), F32),
            pltpu.VMEM((PAGE, slots), F32),
            pltpu.VMEM((pages, 2 * QK), BF16),
            pltpu.VMEM((pages, PAGE), F32),
            pltpu.VMEM((pages, PAGE), F32),
            pltpu.VMEM((pages, VDIM), F32),
            pltpu.VMEM((slots, SHARED * PAGE), BF16),
            dma((4,)),
        ]
        + [dma((count_of,)) for count_of in (7,) * 2 + (n_tok,) * 6 + (7,) * 2 + (n_tok,) * 4 + (7,) * 2],
        compiler_params=pltpu.CompilerParams(
            collective_id=0, has_side_effects=True, vmem_limit_bytes=60 * 1024 * 1024
        ),
        name="decode_step",
    )(
        tokens,
        w_in,
        w_out,
        pool.reshape(pages, PAGE, WIDE),
        gain.reshape(1, VDIM),
        lq1.reshape(1, QK),
        lk1.reshape(1, QK),
        lq2.reshape(1, QK),
        lk2.reshape(1, QK),
        jnp.transpose(table),
        length.reshape(1, count),
        owner.reshape(1, count),
    )


def solution(mesh):
    n_tok, n_head = mesh.shape["tok"], mesh.shape["head"]

    def run(
        tokens,
        input_weight,
        output_weight,
        head_gain,
        query_lambda_one,
        key_lambda_one,
        query_lambda_two,
        key_lambda_two,
        cache_pool,
        page_table,
        cache_length,
        cache_owner,
    ):
        sizes = (n_tok, n_head, tokens.shape[0] // n_tok, tokens.shape[1] // n_head)
        placed = (
            P("tok", "head"),
            P(None, "head"),
            P("head", None),
            P("head"),
            P(),
            P(),
            P(),
            P(),
            P("tok", "head", None, None),
            P("tok", None),
            P("tok"),
            P("tok", None),
        )
        return jax.shard_map(
            functools.partial(on_device, sizes),
            mesh=mesh,
            in_specs=placed,
            out_specs=P("tok", "head"),
            check_vma=False,
        )(
            tokens,
            input_weight,
            output_weight,
            head_gain,
            query_lambda_one,
            key_lambda_one,
            query_lambda_two,
            key_lambda_two,
            cache_pool,
            page_table,
            cache_length,
            cache_owner,
        )

    return run
```

time: 57.5 us -> 50 us (0.87)
  Pallas kernels: 52.8 us -> 48.3 us
  local copies, waits for them, and re-layouts: 4.51 us -> 1.57 us
    pallas_call x1, Pallas kernels: 52.8 us -> 48.3 us  [on_device(): pl.pallas_call(functools.partial(step_kernel, sizes), out_shape=jax.Shape...]
    unnamed x3 -> x1, local copies, waits for them, and re-layouts: 4.51 us -> 1.57 us
where the time goes in v2:
time: 50 us; the launch traced here: 49.8 us
  Pallas kernels  48.3 us (97%)
  local copies, waits for them, and re-layouts  1.57 us (3%)
    pallas_call x1, Pallas kernels, on_device(): pl.pallas_call(functools.partial(step_kernel, sizes), out_shape=jax.Shape...  48.3 us
    unnamed x1, local copies, waits for them, and re-layouts  1.57 us

profile of v2, /device:TPU:1, one launch (start us, length us, event | category | flops | bytes accessed | tf_op | source)
XLA Modules:
  0.0 49.8 jit_solution(4650970497974968120)
XLA Ops:
  0.0 48.3 %decode_step.1 = bf16[256,256]{1,0:T(8,128)(2,1)} custom-call(bf16[256,256]{1,0:T(8,128)(2,1)} %tokens.1, bf16[2048,768]{1,0:T(8,128)(2,1)} %w_in.1, bf16[256,2048]{1,0:T(8,128)(2,1)} %w_out.1, bf16[64,128,512]{2,1,0:T(8,128)(2,1)} %bitcast.9, f32[1,256]{1,0:T(1,128)} %bitcast.11, f32[1,128]{1,0:T(1,128)} %bitcast.14, f32[1,128]{1,0:T(1,128)} %bitcast.15, ...), custom_call_target="tpu_custom_call" | custom-call | tf_op jit(solution)/shard_map/decode_step/pallas_call | solution.py:476
  48.3 1.6 %copy.14 = bf16[256,256]{1,0:T(8,128)(2,1)} copy(bf16[256,256]{1,0:T(8,128)(2,1)} %decode_step.1) | data formatting | bytes 262144

commit v3 on v2

--- a/solution.py
+++ b/solution.py
@@ -113,18 +113,12 @@
     local_sem,
     x_send,
     x_recv,
-    m_send,
-    m_recv,
-    q_send,
-    q_recv,
-    s_send,
-    s_recv,
-    w_send,
-    w_recv,
-    c_send,
-    c_recv,
-    r_send,
-    r_recv,
+    m_sem,
+    q_sem,
+    s_sem,
+    w_sem,
+    c_sem,
+    r_sem,
     h_send,
     h_recv,
 ):
@@ -141,15 +135,16 @@
     z_at, x_at = me_t // nx, me_t % nx
     up, down, far = (y + 1) % ny, (y + ny - 1) % ny, (y + 2) % ny
     sib = y * 2 + 1 - core
-    near = (up * 2 + core, down * 2 + core, far * 2 + core)
-    across = (up * 2 + 1 - core, down * 2 + 1 - core, far * 2 + 1 - core)
+    h_up, h_down, h_far = up * 2 + core, down * 2 + core, far * 2 + core
+    a_up, a_down, a_far = up * 2 + 1 - core, down * 2 + 1 - core, far * 2 + 1 - core
+    others = (sib, h_up, h_down, h_far, a_up, a_down, a_far)
 
     offsets = [(dz, dx) for dz in range(nz) for dx in range(nx) if dz + dx > 0]
     offsets.sort(key=lambda o: -(min(o[0], nz - o[0]) + min(o[1], nx - o[1])))
     peers = [((z_at + dz) % nz) * nx + (x_at + dx) % nx for dz, dx in offsets]
 
     barrier = pltpu.get_barrier_semaphore()
-    for peer in (sib,) + near + across:
+    for peer in others:
         pl.semaphore_signal(barrier, inc=1, device_id=(me_t, peer), device_id_type=MESH)
     for peer in peers:
         pl.semaphore_signal(barrier, inc=1, device_id=(peer, me_h), device_id_type=MESH)
@@ -166,16 +161,26 @@
             device_id_type=MESH,
         )
         copy.start()
+        return copy
+
+    def bulk(source, target, blocks_of, send_sem, recv_sem):
+        some = pl.ds(0, blocks_of)
+        copy = pltpu.make_async_remote_copy(
+            src_ref=source.at[some],
+            dst_ref=target.at[some],
+            send_sem=send_sem,
+            recv_sem=recv_sem,
+            device_id=(me_t, sib),
+            device_id_type=MESH,
+        )
         sent.append(copy)
         return copy
 
-    def exchange(source, target, send_sem, recv_sem):
-        copies = [
-            remote(source.at[p], target.at[me_t], send_sem.at[k], recv_sem.at[k], (p, me_h))
-            for k, p in enumerate(peers)
-        ]
+    def exchange(source, target, sems):
+        for p in peers:
+            remote(source.at[p], target.at[me_t], sems.at[0], sems.at[1], (p, me_h))
         target[me_t] = source[me_t]
-        return copies
+        return bulk(source, target, len(peers), sems.at[0], sems.at[1])
 
     local_x = pltpu.make_async_copy(tokens, x.at[me_h], local_sem.at[0])
     local_x.start()
@@ -218,88 +223,108 @@
     fields = jnp.concatenate([table[...].astype(F32), ends], axis=0).astype(BF16)
     tiles(dot(fields, place_t[...]), FIELDS, send_m)
 
-    pl.semaphore_wait(barrier, 1 + 2 * len(near) + len(peers))
+    pl.semaphore_wait(barrier, len(others) + len(peers))
+
+    quarter = count // 4
 
     def gather_start(buffer, send_sem, recv_sem):
-        def share(index, source, target):
-            return remote(
-                buffer.at[source],
-                buffer.at[source],
-                send_sem.at[index],
-                recv_sem.at[index],
-                (me_t, target),
-            )
-
-        direct = [share(k, me_h, target) for k, target in enumerate(near)]
-        return share, direct, share(3, me_h, sib)
+        def go(index, source, start, quarters, target):
+            part = buffer.at[source, pl.ds(start * quarter, quarters * quarter)]
+            return remote(part, part, send_sem.at[0], recv_sem.at[index], (me_t, target))
+
+        copies = [
+            go(0, me_h, 0, 1, h_up),
+            go(1, me_h, 3, 1, h_down),
+            go(2, me_h, 1, 1, h_up),
+            go(3, me_h, 2, 1, h_down),
+            go(4, me_h, 2, 2, h_up),
+            go(5, me_h, 0, 2, h_down),
+            go(6, me_h, 0, 4, sib),
+        ]
+        bulk(buffer, buffer, n_head - 1, send_sem.at[0], recv_sem.at[0])
+        return go, copies
 
     def gather_rest(started, add):
-        share, direct, twin = started
+        go, copies = started
         add(me_h)
-        twin.wait_recv()
+        for k, (source, start, target) in enumerate(
+            ((h_down, 0, h_up), (h_up, 3, h_down), (h_down, 1, h_up), (h_up, 2, h_down))
+        ):
+            copies[k].wait_recv()
+            copies.append(go(7 + k, source, start, 1, target))
+        copies.append(go(11, h_down, 0, 2, sib))
+        copies.append(go(12, h_up, 2, 2, sib))
+        copies[6].wait_recv()
         add(sib)
-        passed = []
-        for k, turned in enumerate((1, 0, 2)):
-            direct[k].wait_recv()
-            passed.append(share(4 + k, near[turned], sib))
-            add(near[turned])
-            if k > 0:
-                passed[k - 1].wait_recv()
-                add(across[(1, 0, 2)[k - 1]])
-        passed[2].wait_recv()
-        add(across[2])
+        copies[4].wait_recv()
+        copies.append(go(13, h_down, 2, 2, sib))
+        add(h_down)
+        copies[5].wait_recv()
+        copies.append(go(14, h_up, 0, 2, sib))
+        add(h_up)
+        copies[11].wait_recv()
+        copies[13].wait_recv()
+        add(a_down)
+        copies[12].wait_recv()
+        copies[14].wait_recv()
+        add(a_up)
+        for k, start in enumerate((0, 3, 1, 2)):
+            copies[7 + k].wait_recv()
+            copies.append(go(15 + k, h_far, start, 1, sib))
+        add(h_far)
+        for k in range(4):
+            copies[15 + k].wait_recv()
+        add(a_far)
 
     local_x.wait()
     started = gather_start(x, x_send, x_recv)
-    m_copies = exchange(send_m, recv_m, m_send, m_recv)
+    meta_in = exchange(send_m, recv_m, m_sem)
     load_win.wait()
     load_pool = pltpu.make_async_copy(pool, pool_v, local_sem.at[2])
     load_pool.start()
 
-    def add_proj(source):
+    def add_query(source):
         rows = pl.ds(pl.multiple_of(source * features, features), features)
-        update = dot(x[source], win_v[rows, 0 : 4 * QK])
-        proj[...] = proj[...] + update
+        proj[...] = proj[...] + dot(x[source], win_v[rows, 0 : 2 * QK])
 
     proj[...] = jnp.zeros(proj.shape, F32)
-    gather_rest(started, add_proj)
-
-    qk = proj[...].astype(BF16)
-    send_q[...] = dot(place[...], qk[:, 0 : 2 * QK]).astype(BF16).reshape(n_tok, CAP, 2 * QK)
-    q_copies = exchange(send_q, recv_q, q_send, q_recv)
-    qf = qk.astype(F32)
+    gather_rest(started, add_query)
+
+    query = proj[...].astype(BF16)
+    send_q[...] = dot(place[...], query).astype(BF16).reshape(n_tok, CAP, 2 * QK)
+    query_in = exchange(send_q, recv_q, q_sem)
+
+    fresh = jnp.zeros((count, 2 * QK + VDIM), F32)
+    for h in range(n_head):
+        fresh = fresh + dot(x[h], win_v[h * features : (h + 1) * features, 2 * QK :])
+    fresh = fresh.astype(BF16)
+    v_new[...] = fresh[:, 2 * QK :]
+    product = query.astype(F32) * fresh[:, 0 : 2 * QK].astype(F32)
+    high, low = split(product, 2)
     ones = jnp.ones((8, QK), F32).astype(BF16)
     terms = []
     for m in range(2):
-        product = qf[:, m * QK : (m + 1) * QK] * qf[:, (m + 2) * QK : (m + 3) * QK]
-        high, low = split(product, 2)
-        total = dot_nt(ones, high.astype(BF16)) + dot_nt(ones, low.astype(BF16))
+        part = slice(m * QK, (m + 1) * QK)
+        total = dot_nt(ones, high[:, part].astype(BF16)) + dot_nt(ones, low[:, part].astype(BF16))
         terms += split(total[0:1] * SCALE, 3)
     tiles(dot(stack_rows(terms, TILE).astype(BF16), place_t[...]), TILE, send_s)
-    s_copies = exchange(send_s, recv_s, s_send, s_recv)
+    self_in = exchange(send_s, recv_s, s_sem)
 
     def columns(h):
         return w_out.at[:, pl.ds(pl.multiple_of(h * features, features), features)]
 
     own_w = pltpu.make_async_copy(columns(me_h), wcol_v.at[me_h], local_sem.at[3])
     own_w.start()
-    w_copies = [
-        remote(columns(h), wcol_v.at[me_h], w_send.at[k], w_recv.at[k], (me_t, h))
-        for k, h in enumerate(near + across + (sib,))
-    ]
-
-    value = jnp.zeros((count, VDIM), F32)
-    for h in range(n_head):
-        value = value + dot(x[h], win_v[h * features : (h + 1) * features, 4 * QK :])
-    v_new[...] = value.astype(BF16)
+    for h in (h_up, h_down, h_far, a_up, a_down, a_far, sib):
+        remote(columns(h), wcol_v.at[me_h], w_sem.at[0], w_sem.at[1], (me_t, h))
+    weights_in = bulk(wcol_v, wcol_v, n_head - 1, w_sem.at[0], w_sem.at[1])
     lam = (
         jnp.exp(jnp.sum(lq1[...] * lk1[...], axis=1, keepdims=True))
         - jnp.exp(jnp.sum(lq2[...] * lk2[...], axis=1, keepdims=True))
         + lambda_init
     )
 
-    for copy in m_copies:
-        copy.wait_recv()
+    meta_in.wait_recv()
     whole = jnp.zeros((pages, LANES), F32)
     rest = jnp.zeros((pages, LANES), F32)
     page = iota((pages, LANES), 0).astype(F32)
@@ -327,8 +352,7 @@
     position = iota((pages, PAGE), 1).astype(F32)
     times[...] = whole + jnp.where(position < rest, 1.0, 0.0)
     load_pool.wait()
-    for copy in q_copies:
-        copy.wait_recv()
+    query_in.wait_recv()
 
     queries = recv_q[...].reshape(slots, 2 * QK)
     page_q[...] = dot(match[...], queries).astype(BF16)
@@ -360,8 +384,7 @@
 
     lax.fori_loop(0, pages // GROUP, private_scores, 0)
 
-    for copy in s_copies:
-        copy.wait_recv()
+    self_in.wait_recv()
     page_best = []
     for ref in (priv_a, priv_b):
         score = jnp.where(times[...] > 0.0, ref[...] * SCALE, NEG)
@@ -415,7 +438,7 @@
             wide[cut, p * PAGE : (p + 1) * PAGE] = mixed * page0[p, cut]
         own_rows.append(stack_rows(split(own_coef, 2), TILE))
     tiles(jnp.concatenate(own_rows, axis=1), TILE, send_c)
-    c_copies = exchange(send_c, recv_c, c_send, c_recv)
+    coef_in = exchange(send_c, recv_c, c_sem)
 
     priv_a[...] = priv_a[...] * jnp.sum(page_coef[0], axis=1, keepdims=True) + priv_b[
         ...
@@ -438,30 +461,26 @@
     result = dot(wide[...], values) + dot(match_t[...], pair)
     send_r[...] = result.astype(BF16).reshape(n_tok, CAP, VDIM)
 
-    r_copies = exchange(send_r, recv_r, r_send, r_recv)
+    mixed_in = exchange(send_r, recv_r, r_sem)
     own_w.wait()
-    for copy in c_copies:
-        copy.wait_recv()
+    coef_in.wait_recv()
     rows = jnp.concatenate([gather_tiles(recv_c, g) for g in range(blocks)], axis=1)
     coefs = dot_nt(place_t[...], rows.astype(BF16))
     addend = (coefs[:, 0:1] + coefs[:, 1:2]) * v_new[...].astype(F32)
-    for copy in r_copies:
-        copy.wait_recv()
+    mixed_in.wait_recv()
     mixed = dot(place_t[...], recv_r[...].reshape(slots, VDIM)) + addend
     scale = lax.rsqrt(jnp.mean(mixed * mixed, axis=1, keepdims=True) + norm_eps)
     heads[me_h] = (mixed * scale * gain[...] * (1.0 - lambda_init)).astype(BF16)
 
     started = gather_start(heads, h_send, h_recv)
-    for copy in w_copies:
-        copy.wait_recv()
-    mix = proj.at[:, 0:features]
-    mix[...] = jnp.zeros(mix.shape, F32)
+    weights_in.wait_recv()
+    proj[...] = jnp.zeros(proj.shape, F32)
 
     def add_out(source):
-        mix[...] = mix[...] + dot(heads[source], wcol_v[source])
+        proj[...] = proj[...] + dot(heads[source], wcol_v[source])
 
     gather_rest(started, add_out)
-    out[...] = mix[...].astype(BF16)
+    out[...] = proj[...].astype(BF16)
     for copy in sent:
         copy.wait_send()
 
@@ -487,7 +506,7 @@
             pltpu.VMEM((slots, count), BF16),
             pltpu.VMEM((count, slots), BF16),
             pltpu.VMEM((PER, LANES, LANES), BF16),
-            pltpu.VMEM((count, 4 * QK), F32),
+            pltpu.VMEM((count, 2 * QK), F32),
             pltpu.VMEM((count, VDIM), BF16),
             pltpu.VMEM((n_tok, FIELDS, LANES), BF16),
             pltpu.VMEM((n_tok, FIELDS, LANES), BF16),
@@ -513,7 +532,7 @@
             pltpu.VMEM((slots, SHARED * PAGE), BF16),
             dma((4,)),
         ]
-        + [dma((count_of,)) for count_of in (7,) * 2 + (n_tok,) * 6 + (7,) * 2 + (n_tok,) * 4 + (7,) * 2],
+        + [dma((number,)) for number in (1, 19, 2, 2, 2, 2, 2, 2, 1, 19)],
         compiler_params=pltpu.CompilerParams(
             collective_id=0, has_side_effects=True, vmem_limit_bytes=60 * 1024 * 1024
         ),

time: 50 us -> 46.8 us (0.936)
  Pallas kernels: 48.3 us -> 45.1 us
    pallas_call x1, Pallas kernels: 48.3 us -> 45.1 us  [on_device(): pl.pallas_call(functools.partial(step_kernel, sizes), out_shape=jax.Shape...]
where the time goes in v3:
time: 46.8 us; the launch traced here: 46.7 us
  Pallas kernels  45.1 us (96%)
  local copies, waits for them, and re-layouts  1.57 us (3%)
    pallas_call x1, Pallas kernels, on_device(): pl.pallas_call(functools.partial(step_kernel, sizes), out_shape=jax.Shape...  45.1 us
    unnamed x1, local copies, waits for them, and re-layouts  1.57 us

profile of v3, /device:TPU:1, one launch (start us, length us, event | category | flops | bytes accessed | tf_op | source)
XLA Modules:
  0.0 46.7 jit_solution(9477633443120255159)
XLA Ops:
  0.0 45.1 %decode_step.1 = bf16[256,256]{1,0:T(8,128)(2,1)} custom-call(bf16[256,256]{1,0:T(8,128)(2,1)} %tokens.1, bf16[2048,768]{1,0:T(8,128)(2,1)} %w_in.1, bf16[256,2048]{1,0:T(8,128)(2,1)} %w_out.1, bf16[64,128,512]{2,1,0:T(8,128)(2,1)} %bitcast.9, f32[1,256]{1,0:T(1,128)} %bitcast.11, f32[1,128]{1,0:T(1,128)} %bitcast.14, f32[1,128]{1,0:T(1,128)} %bitcast.15, ...), custom_call_target="tpu_custom_call" | custom-call | tf_op jit(solution)/shard_map/decode_step/pallas_call | solution.py:495
  45.1 1.6 %copy.14 = bf16[256,256]{1,0:T(8,128)(2,1)} copy(bf16[256,256]{1,0:T(8,128)(2,1)} %decode_step.1) | data formatting | bytes 262144

commit v4 on v3

--- a/solution.py
+++ b/solution.py
@@ -69,6 +69,15 @@
     w_in,
     w_out,
     pool,
+    gain_h,
+    lq1_h,
+    lk1_h,
+    lq2_h,
+    lk2_h,
+    table_h,
+    length_h,
+    owner_h,
+    out,
     gain,
     lq1,
     lk1,
@@ -77,7 +86,6 @@
     table,
     length,
     owner,
-    out,
     x,
     win_v,
     wcol_v,
@@ -187,6 +195,26 @@
     load_win = pltpu.make_async_copy(w_in, win_v, local_sem.at[1])
     load_win.start()
 
+    small = [
+        pltpu.make_async_copy(source, target, local_sem.at[4 + k])
+        for k, (source, target) in enumerate(
+            (
+                (owner_h, owner),
+                (table_h, table),
+                (length_h, length),
+                (gain_h, gain),
+                (lq1_h, lq1),
+                (lk1_h, lk1),
+                (lq2_h, lq2),
+                (lk2_h, lk2),
+            )
+        )
+    ]
+    for load in small:
+        load.start()
+    for load in small:
+        load.wait()
+
     own = owner[...]
     named = own == iota((n_tok, count), 0)
     earlier = one_hot(iota((count, count), 0) < iota((count, count), 1))
@@ -355,7 +383,12 @@
     query_in.wait_recv()
 
     queries = recv_q[...].reshape(slots, 2 * QK)
-    page_q[...] = dot(match[...], queries).astype(BF16)
+    found = dot(match[...], queries)
+    side = iota((GROUP, 2 * QK), 1) < QK
+    for g in range(pages // GROUP):
+        mine = found[g * GROUP : (g + 1) * GROUP]
+        both = [jnp.where(side, mine, 0.0), jnp.where(side, 0.0, mine)]
+        page_q[2 * g * GROUP : 2 * (g + 1) * GROUP] = jnp.concatenate(both, axis=0).astype(BF16)
     half = slots // 2
     for h in range(2):
         cut = slice(h * half, (h + 1) * half)
@@ -369,20 +402,16 @@
                 kept = chosen if p == 0 else jnp.where(at >= float(p), chosen, kept)
             ref[:, cut] = kept
 
-    row = iota((GROUP, LANES), 0)
-
-    def private_scores(g, carry):
-        mine = pl.ds(pl.multiple_of(g * GROUP, GROUP), GROUP)
-        keys = pool_v[mine].reshape(GROUP * PAGE, WIDE)
-        for ref, lo in ((priv_a, 0), (priv_b, QK)):
-            score = dot_nt(page_q[mine, lo : lo + QK], keys[:, lo : lo + QK])
-            chosen = score[:, 0:PAGE]
-            for i in range(1, GROUP):
-                chosen = jnp.where(row == i, score[:, i * PAGE : (i + 1) * PAGE], chosen)
-            ref[mine] = chosen
-        return carry
-
-    lax.fori_loop(0, pages // GROUP, private_scores, 0)
+    row = iota((2 * GROUP, LANES), 0) % GROUP
+    for g in range(pages // GROUP):
+        mine = slice(g * GROUP, (g + 1) * GROUP)
+        keys = pool_v[mine].reshape(GROUP * PAGE, WIDE)[:, 0 : 2 * QK]
+        score = dot_nt(page_q[2 * g * GROUP : 2 * (g + 1) * GROUP], keys)
+        chosen = score[:, 0:PAGE]
+        for i in range(1, GROUP):
+            chosen = jnp.where(row == i, score[:, i * PAGE : (i + 1) * PAGE], chosen)
+        priv_a[mine] = chosen[0:GROUP]
+        priv_b[mine] = chosen[GROUP:]
 
     self_in.wait_recv()
     page_best = []
@@ -444,17 +473,15 @@
         ...
     ] * jnp.sum(page_coef[1], axis=1, keepdims=True)
 
-    def private_values(g, carry):
-        mine = pl.ds(pl.multiple_of(g * GROUP, GROUP), GROUP)
+    row = iota((GROUP, LANES), 0)
+    for g in range(pages // GROUP):
+        mine = slice(g * GROUP, (g + 1) * GROUP)
         values = pool_v[mine].reshape(GROUP * PAGE, WIDE)[:, 2 * QK :]
         weight = priv_a[mine]
         spread = jnp.concatenate(
             [jnp.where(row == i, weight, 0.0) for i in range(GROUP)], axis=1
         ).astype(BF16)
         page_out[mine] = dot(spread, values)
-        return carry
-
-    lax.fori_loop(0, pages // GROUP, private_values, 0)
     high, low = split(page_out[...], 2)
     pair = jnp.concatenate([high, low], axis=0).astype(BF16)
     values = pool_v[0:SHARED].reshape(SHARED * PAGE, WIDE)[:, 2 * QK :]
@@ -490,14 +517,22 @@
     slots = n_tok * CAP
     pages = pool.shape[0]
     vmem = pl.BlockSpec(memory_space=pltpu.VMEM)
-    hbm = pl.BlockSpec(memory_space=pl.ANY)
+    hbm = pl.BlockSpec(memory_space=pltpu.HBM)
     dma = pltpu.SemaphoreType.DMA
     return pl.pallas_call(
         functools.partial(step_kernel, sizes),
-        out_shape=jax.ShapeDtypeStruct((count, features), BF16),
-        in_specs=[hbm] * 4 + [vmem] * 8,
+        out_shape=pltpu.VMEM((count, features), BF16),
+        in_specs=[hbm] * 12,
         out_specs=vmem,
         scratch_shapes=[
+            pltpu.VMEM((1, VDIM), F32),
+            pltpu.VMEM((1, QK), F32),
+            pltpu.VMEM((1, QK), F32),
+            pltpu.VMEM((1, QK), F32),
+            pltpu.VMEM((1, QK), F32),
+            pltpu.VMEM((MAXP, count), jnp.int32),
+            pltpu.VMEM((1, count), jnp.int32),
+            pltpu.VMEM((1, count), jnp.int32),
             pltpu.VMEM((n_head, count, features), BF16),
             pltpu.VMEM(w_in.shape, BF16),
             pltpu.VMEM((n_head, VDIM, features), BF16),
@@ -525,12 +560,12 @@
             pltpu.VMEM((SHARED, slots, PAGE), BF16),
             pltpu.VMEM((PAGE, slots), F32),
             pltpu.VMEM((PAGE, slots), F32),
-            pltpu.VMEM((pages, 2 * QK), BF16),
+            pltpu.VMEM((2 * pages, 2 * QK), BF16),
             pltpu.VMEM((pages, PAGE), F32),
             pltpu.VMEM((pages, PAGE), F32),
             pltpu.VMEM((pages, VDIM), F32),
             pltpu.VMEM((slots, SHARED * PAGE), BF16),
-            dma((4,)),
+            dma((12,)),
         ]
         + [dma((number,)) for number in (1, 19, 2, 2, 2, 2, 2, 2, 1, 19)],
         compiler_params=pltpu.CompilerParams(

time: 46.8 us -> 43.8 us (0.936)
  Pallas kernels: 45.1 us -> 43.1 us
  local copies, waits for them, and re-layouts: 1.57 us -> 0.66 us
    pallas_call x1, Pallas kernels: 45.1 us -> 43.1 us  [on_device(): pl.pallas_call(functools.partial(step_kernel, sizes), out_shape=pltpu.VME...]
    unnamed x1, local copies, waits for them, and re-layouts: 1.57 us -> 0.66 us
where the time goes in v4:
time: 43.8 us; the launch traced here: 43.7 us
  Pallas kernels  43.1 us (98%)
  local copies, waits for them, and re-layouts  0.66 us (2%)
    pallas_call x1, Pallas kernels, on_device(): pl.pallas_call(functools.partial(step_kernel, sizes), out_shape=pltpu.VME...  43.1 us

profile of v4, /device:TPU:1, one launch (start us, length us, event | category | flops | bytes accessed | tf_op | source)
XLA Modules:
  0.0 43.7 jit_solution(16578972050065422052)
XLA Ops:
  0.0 43.1 %decode_step.1 = bf16[256,256]{1,0:T(8,128)(2,1)S(1)} custom-call(bf16[256,256]{1,0:T(8,128)(2,1)} %tokens.1, bf16[2048,768]{1,0:T(8,128)(2,1)} %w_in.1, bf16[256,2048]{1,0:T(8,128)(2,1)} %w_out.1, bf16[64,128,512]{2,1,0:T(8,128)(2,1)} %bitcast.9, f32[1,256]{1,0:T(1,128)} %bitcast.11, f32[1,128]{1,0:T(1,128)} %bitcast.14, f32[1,128]{1,0:T(1,128)} %bitcast.15, ...), custom_call_target="tpu_custom_call" | custom-call | tf_op jit(solution)/shard_map/decode_step/pallas_call | solution.py:522
  43.1 0.7 %copy.14 = bf16[256,256]{1,0:T(8,128)(2,1)} copy(bf16[256,256]{1,0:T(8,128)(2,1)S(1)} %decode_step.1) | data formatting | bytes 262144

commit v5 on v4

--- a/solution.py
+++ b/solution.py
@@ -118,6 +118,7 @@
     priv_b,
     page_out,
     wide,
+    greet_sem,
     local_sem,
     x_send,
     x_recv,
@@ -145,17 +146,27 @@
     sib = y * 2 + 1 - core
     h_up, h_down, h_far = up * 2 + core, down * 2 + core, far * 2 + core
     a_up, a_down, a_far = up * 2 + 1 - core, down * 2 + 1 - core, far * 2 + 1 - core
-    others = (sib, h_up, h_down, h_far, a_up, a_down, a_far)
 
     offsets = [(dz, dx) for dz in range(nz) for dx in range(nx) if dz + dx > 0]
     offsets.sort(key=lambda o: -(min(o[0], nz - o[0]) + min(o[1], nx - o[1])))
     peers = [((z_at + dz) % nz) * nx + (x_at + dx) % nx for dz, dx in offsets]
 
     barrier = pltpu.get_barrier_semaphore()
-    for peer in others:
+    x_near = [z_at * nx + (x_at + d) % nx for d in (1, nx - 1)]
+    z_near = [(z_at + d) % nz * nx + x_at for d in (1, nz - 1)]
+    for peer in (sib, h_up, h_down):
         pl.semaphore_signal(barrier, inc=1, device_id=(me_t, peer), device_id_type=MESH)
-    for peer in peers:
+    for peer in x_near + z_near:
         pl.semaphore_signal(barrier, inc=1, device_id=(peer, me_h), device_id_type=MESH)
+
+    def greet(step):
+        if step > 0:
+            pl.semaphore_wait(greet_sem.at[step - 1], 2)
+        if step < 3:
+            for peer in (x_near, z_near, z_near)[step]:
+                pl.semaphore_signal(
+                    greet_sem.at[step], inc=1, device_id=(peer, me_h), device_id_type=MESH
+                )
 
     sent = []
 
@@ -251,7 +262,7 @@
     fields = jnp.concatenate([table[...].astype(F32), ends], axis=0).astype(BF16)
     tiles(dot(fields, place_t[...]), FIELDS, send_m)
 
-    pl.semaphore_wait(barrier, len(others) + len(peers))
+    pl.semaphore_wait(barrier, 3 + len(x_near) + len(z_near))
 
     quarter = count // 4
 
@@ -272,7 +283,7 @@
         bulk(buffer, buffer, n_head - 1, send_sem.at[0], recv_sem.at[0])
         return go, copies
 
-    def gather_rest(started, add):
+    def gather_rest(started, add, beside):
         go, copies = started
         add(me_h)
         for k, (source, start, target) in enumerate(
@@ -282,6 +293,7 @@
             copies.append(go(7 + k, source, start, 1, target))
         copies.append(go(11, h_down, 0, 2, sib))
         copies.append(go(12, h_up, 2, 2, sib))
+        beside(1)
         copies[6].wait_recv()
         add(sib)
         copies[4].wait_recv()
@@ -290,6 +302,7 @@
         copies[5].wait_recv()
         copies.append(go(14, h_up, 0, 2, sib))
         add(h_up)
+        beside(2)
         copies[11].wait_recv()
         copies[13].wait_recv()
         add(a_down)
@@ -299,6 +312,7 @@
         for k, start in enumerate((0, 3, 1, 2)):
             copies[7 + k].wait_recv()
             copies.append(go(15 + k, h_far, start, 1, sib))
+        beside(3)
         add(h_far)
         for k in range(4):
             copies[15 + k].wait_recv()
@@ -306,7 +320,7 @@
 
     local_x.wait()
     started = gather_start(x, x_send, x_recv)
-    meta_in = exchange(send_m, recv_m, m_sem)
+    greet(0)
     load_win.wait()
     load_pool = pltpu.make_async_copy(pool, pool_v, local_sem.at[2])
     load_pool.start()
@@ -316,7 +330,14 @@
         proj[...] = proj[...] + dot(x[source], win_v[rows, 0 : 2 * QK])
 
     proj[...] = jnp.zeros(proj.shape, F32)
-    gather_rest(started, add_query)
+    arriving = []
+
+    def beside_gather(step):
+        greet(step)
+        if step == 3:
+            arriving.append(exchange(send_m, recv_m, m_sem))
+
+    gather_rest(started, add_query, beside_gather)
 
     query = proj[...].astype(BF16)
     send_q[...] = dot(place[...], query).astype(BF16).reshape(n_tok, CAP, 2 * QK)
@@ -352,7 +373,7 @@
         + lambda_init
     )
 
-    meta_in.wait_recv()
+    arriving[0].wait_recv()
     whole = jnp.zeros((pages, LANES), F32)
     rest = jnp.zeros((pages, LANES), F32)
     page = iota((pages, LANES), 0).astype(F32)
@@ -506,7 +527,7 @@
     def add_out(source):
         proj[...] = proj[...] + dot(heads[source], wcol_v[source])
 
-    gather_rest(started, add_out)
+    gather_rest(started, add_out, lambda step: None)
     out[...] = proj[...].astype(BF16)
     for copy in sent:
         copy.wait_send()
@@ -565,6 +586,7 @@
             pltpu.VMEM((pages, PAGE), F32),
             pltpu.VMEM((pages, VDIM), F32),
             pltpu.VMEM((slots, SHARED * PAGE), BF16),
+            pltpu.SemaphoreType.REGULAR((3,)),
             dma((12,)),
         ]
         + [dma((number,)) for number in (1, 19, 2, 2, 2, 2, 2, 2, 1, 19)],

time: 43.8 us -> 43 us (0.982)
  Pallas kernels: 43.1 us -> 42.2 us
    pallas_call x1, Pallas kernels: 43.1 us -> 42.2 us  [on_device(): pl.pallas_call(functools.partial(step_kernel, sizes), out_shape=pltpu.VME...]
where the time goes in v5:
time: 43 us; the launch traced here: 42.9 us
  Pallas kernels  42.2 us (98%)
  local copies, waits for them, and re-layouts  0.66 us (2%)
    pallas_call x1, Pallas kernels, on_device(): pl.pallas_call(functools.partial(step_kernel, sizes), out_shape=pltpu.VME...  42.2 us

profile of v5, /device:TPU:1, one launch (start us, length us, event | category | flops | bytes accessed | tf_op | source)
XLA Modules:
  0.0 42.9 jit_solution(8538009311806230843)
XLA Ops:
  0.0 42.2 %decode_step.1 = bf16[256,256]{1,0:T(8,128)(2,1)S(1)} custom-call(bf16[256,256]{1,0:T(8,128)(2,1)} %tokens.1, bf16[2048,768]{1,0:T(8,128)(2,1)} %w_in.1, bf16[256,2048]{1,0:T(8,128)(2,1)} %w_out.1, bf16[64,128,512]{2,1,0:T(8,128)(2,1)} %bitcast.9, f32[1,256]{1,0:T(1,128)} %bitcast.11, f32[1,128]{1,0:T(1,128)} %bitcast.14, f32[1,128]{1,0:T(1,128)} %bitcast.15, ...), custom_call_target="tpu_custom_call" | custom-call | tf_op jit(solution)/shard_map/decode_step/pallas_call | solution.py:543
  42.2 0.7 %copy.14 = bf16[256,256]{1,0:T(8,128)(2,1)} copy(bf16[256,256]{1,0:T(8,128)(2,1)S(1)} %decode_step.1) | data formatting | bytes 262144

commit v6 on v5

--- a/solution.py
+++ b/solution.py
@@ -201,6 +201,18 @@
         target[me_t] = source[me_t]
         return bulk(source, target, len(peers), sems.at[0], sems.at[1])
 
+    def exchange_rows(make, source, target, sems):
+        for dz in sorted(range(nz), key=lambda d: -min(d, nz - d)):
+            zz = (z_at + dz) % nz
+            rows = pl.ds(pl.multiple_of(zz * nx * CAP, nx * CAP), nx * CAP)
+            source[pl.ds(zz * nx, nx)] = make(rows).astype(BF16).reshape((nx,) + source.shape[1:])
+            for dx in sorted(range(nx), key=lambda d: -min(d, nx - d)):
+                if dz + dx > 0:
+                    p = zz * nx + (x_at + dx) % nx
+                    remote(source.at[p], target.at[me_t], sems.at[0], sems.at[1], (p, me_h))
+        target[me_t] = source[me_t]
+        return bulk(source, target, len(peers), sems.at[0], sems.at[1])
+
     local_x = pltpu.make_async_copy(tokens, x.at[me_h], local_sem.at[0])
     local_x.start()
     load_win = pltpu.make_async_copy(w_in, win_v, local_sem.at[1])
@@ -223,53 +235,16 @@
     ]
     for load in small:
         load.start()
-    for load in small:
-        load.wait()
-
-    own = owner[...]
-    named = own == iota((n_tok, count), 0)
-    earlier = one_hot(iota((count, count), 0) < iota((count, count), 1))
-    before = dot(one_hot(named), earlier)
-    rank = jnp.sum(jnp.where(named, before, 0.0), axis=0, keepdims=True)
-    slot = own * CAP + rank.astype(jnp.int32)
-    eye = iota((count, count), 0) == iota((count, count), 1)
-    slot_c = jnp.sum(jnp.where(eye, slot, 0), axis=1, keepdims=True)
-    place[...] = one_hot(iota((slots, count), 0) == slot)
-    place_t[...] = one_hot(iota((count, slots), 1) == slot_c)
-    shift = (me_t % PER) * CAP
-    for b in range(PER):
-        source_lane = iota((LANES, LANES), 0)
-        moved = source_lane - b * CAP + shift == iota((LANES, LANES), 1)
-        turn[b] = one_hot(moved & (source_lane // CAP == b))
-
-    def tiles(rows, height, target):
-        groups = jnp.concatenate(
-            [rows[:, g * LANES : (g + 1) * LANES] for g in range(blocks)], axis=0
-        ).astype(BF16)
-        for b in range(PER):
-            moved = dot(groups, turn[b]).astype(BF16)
-            for g in range(blocks):
-                target[g * PER + b] = moved[g * height : (g + 1) * height]
-
-    def gather_tiles(source, g):
-        total = source[g * PER].astype(F32)
-        for b in range(1, PER):
-            total = total + source[g * PER + b].astype(F32)
-        return total
-
-    lengths = length[...]
-    ends = stack_rows([(lengths // 8).astype(F32), (lengths % 8).astype(F32)], 8)
-    fields = jnp.concatenate([table[...].astype(F32), ends], axis=0).astype(BF16)
-    tiles(dot(fields, place_t[...]), FIELDS, send_m)
-
     pl.semaphore_wait(barrier, 3 + len(x_near) + len(z_near))
 
     quarter = count // 4
 
-    def gather_start(buffer, send_sem, recv_sem):
+    def gather_start(buffer, mine, send_sem, recv_sem):
         def go(index, source, start, quarters, target):
-            part = buffer.at[source, pl.ds(start * quarter, quarters * quarter)]
-            return remote(part, part, send_sem.at[0], recv_sem.at[index], (me_t, target))
+            rows = pl.ds(start * quarter, quarters * quarter)
+            part = buffer.at[source, rows]
+            origin = mine.at[rows] if source is me_h else part
+            return remote(origin, part, send_sem.at[0], recv_sem.at[index], (me_t, target))
 
         copies = [
             go(0, me_h, 0, 1, h_up),
@@ -285,7 +260,6 @@
 
     def gather_rest(started, add, beside):
         go, copies = started
-        add(me_h)
         for k, (source, start, target) in enumerate(
             ((h_down, 0, h_up), (h_up, 3, h_down), (h_down, 1, h_up), (h_up, 2, h_down))
         ):
@@ -294,6 +268,7 @@
         copies.append(go(11, h_down, 0, 2, sib))
         copies.append(go(12, h_up, 2, 2, sib))
         beside(1)
+        add(me_h)
         copies[6].wait_recv()
         add(sib)
         copies[4].wait_recv()
@@ -318,30 +293,70 @@
             copies[15 + k].wait_recv()
         add(a_far)
 
-    local_x.wait()
-    started = gather_start(x, x_send, x_recv)
+    def tiles(rows, height, target):
+        groups = jnp.concatenate(
+            [rows[:, g * LANES : (g + 1) * LANES] for g in range(blocks)], axis=0
+        ).astype(BF16)
+        for b in range(PER):
+            moved = dot(groups, turn[b]).astype(BF16)
+            for g in range(blocks):
+                target[g * PER + b] = moved[g * height : (g + 1) * height]
+
+    def gather_tiles(source, g):
+        total = source[g * PER].astype(F32)
+        for b in range(1, PER):
+            total = total + source[g * PER + b].astype(F32)
+        return total
+
+    started = gather_start(x, tokens, x_send, x_recv)
     greet(0)
-    load_win.wait()
-    load_pool = pltpu.make_async_copy(pool, pool_v, local_sem.at[2])
-    load_pool.start()
+
+    def prepare():
+        for load in small:
+            load.wait()
+        own = owner[...]
+        named = own == iota((n_tok, count), 0)
+        earlier = one_hot(iota((count, count), 0) < iota((count, count), 1))
+        before = dot(one_hot(named), earlier)
+        rank = jnp.sum(jnp.where(named, before, 0.0), axis=0, keepdims=True)
+        slot = own * CAP + rank.astype(jnp.int32)
+        eye = iota((count, count), 0) == iota((count, count), 1)
+        slot_c = jnp.sum(jnp.where(eye, slot, 0), axis=1, keepdims=True)
+        place[...] = one_hot(iota((slots, count), 0) == slot)
+        place_t[...] = one_hot(iota((count, slots), 1) == slot_c)
+        shift = (me_t % PER) * CAP
+        for b in range(PER):
+            source_lane = iota((LANES, LANES), 0)
+            moved = source_lane - b * CAP + shift == iota((LANES, LANES), 1)
+            turn[b] = one_hot(moved & (source_lane // CAP == b))
+
+        lengths = length[...]
+        ends = stack_rows([(lengths // 8).astype(F32), (lengths % 8).astype(F32)], 8)
+        fields = jnp.concatenate([table[...].astype(F32), ends], axis=0).astype(BF16)
+        tiles(dot(fields, place_t[...]), FIELDS, send_m)
 
     def add_query(source):
         rows = pl.ds(pl.multiple_of(source * features, features), features)
         proj[...] = proj[...] + dot(x[source], win_v[rows, 0 : 2 * QK])
 
     proj[...] = jnp.zeros(proj.shape, F32)
+    load_pool = pltpu.make_async_copy(pool, pool_v, local_sem.at[2])
     arriving = []
 
     def beside_gather(step):
         greet(step)
-        if step == 3:
+        if step == 1:
+            prepare()
+            local_x.wait()
+            load_win.wait()
+            load_pool.start()
+        elif step == 3:
             arriving.append(exchange(send_m, recv_m, m_sem))
 
     gather_rest(started, add_query, beside_gather)
 
     query = proj[...].astype(BF16)
-    send_q[...] = dot(place[...], query).astype(BF16).reshape(n_tok, CAP, 2 * QK)
-    query_in = exchange(send_q, recv_q, q_sem)
+    query_in = exchange_rows(lambda rows: dot(place[rows], query), send_q, recv_q, q_sem)
 
     fresh = jnp.zeros((count, 2 * QK + VDIM), F32)
     for h in range(n_head):
@@ -506,10 +521,10 @@
     high, low = split(page_out[...], 2)
     pair = jnp.concatenate([high, low], axis=0).astype(BF16)
     values = pool_v[0:SHARED].reshape(SHARED * PAGE, WIDE)[:, 2 * QK :]
-    result = dot(wide[...], values) + dot(match_t[...], pair)
-    send_r[...] = result.astype(BF16).reshape(n_tok, CAP, VDIM)
-
-    mixed_in = exchange(send_r, recv_r, r_sem)
+
+    mixed_in = exchange_rows(
+        lambda rows: dot(wide[rows], values) + dot(match_t[rows], pair), send_r, recv_r, r_sem
+    )
     own_w.wait()
     coef_in.wait_recv()
     rows = jnp.concatenate([gather_tiles(recv_c, g) for g in range(blocks)], axis=1)
@@ -520,7 +535,7 @@
     scale = lax.rsqrt(jnp.mean(mixed * mixed, axis=1, keepdims=True) + norm_eps)
     heads[me_h] = (mixed * scale * gain[...] * (1.0 - lambda_init)).astype(BF16)
 
-    started = gather_start(heads, h_send, h_recv)
+    started = gather_start(heads, heads.at[me_h], h_send, h_recv)
     weights_in.wait_recv()
     proj[...] = jnp.zeros(proj.shape, F32)
 

time: 43 us -> 42 us (0.977)
  Pallas kernels: 42.2 us -> 41.3 us
    pallas_call x1, Pallas kernels: 42.2 us -> 41.3 us  [on_device(): pl.pallas_call(functools.partial(step_kernel, sizes), out_shape=pltpu.VME...]
where the time goes in v6:
time: 42 us; the launch traced here: 41.9 us
  Pallas kernels  41.3 us (98%)
  local copies, waits for them, and re-layouts  0.66 us (2%)
    pallas_call x1, Pallas kernels, on_device(): pl.pallas_call(functools.partial(step_kernel, sizes), out_shape=pltpu.VME...  41.3 us

profile of v6, /device:TPU:1, one launch (start us, length us, event | category | flops | bytes accessed | tf_op | source)
XLA Modules:
  0.0 41.9 jit_solution(15054608043293802601)
XLA Ops:
  0.0 41.3 %decode_step.1 = bf16[256,256]{1,0:T(8,128)(2,1)S(1)} custom-call(bf16[256,256]{1,0:T(8,128)(2,1)} %tokens.1, bf16[2048,768]{1,0:T(8,128)(2,1)} %w_in.1, bf16[256,2048]{1,0:T(8,128)(2,1)} %w_out.1, bf16[64,128,512]{2,1,0:T(8,128)(2,1)} %bitcast.9, f32[1,256]{1,0:T(1,128)} %bitcast.11, f32[1,128]{1,0:T(1,128)} %bitcast.14, f32[1,128]{1,0:T(1,128)} %bitcast.15, ...), custom_call_target="tpu_custom_call" | custom-call | tf_op jit(solution)/shard_map/decode_step/pallas_call | solution.py:558
  41.3 0.7 %copy.14 = bf16[256,256]{1,0:T(8,128)(2,1)} copy(bf16[256,256]{1,0:T(8,128)(2,1)S(1)} %decode_step.1) | data formatting | bytes 262144

commit v7 on v6

--- a/solution.py
+++ b/solution.py
@@ -14,7 +14,7 @@
 CAP = 32
 SHARED = 8
 MAXP = 8
-GROUP = 16
+GROUP = 8
 LANES = 128
 FIELDS = 16
 TILE = 8
@@ -213,28 +213,6 @@
         target[me_t] = source[me_t]
         return bulk(source, target, len(peers), sems.at[0], sems.at[1])
 
-    local_x = pltpu.make_async_copy(tokens, x.at[me_h], local_sem.at[0])
-    local_x.start()
-    load_win = pltpu.make_async_copy(w_in, win_v, local_sem.at[1])
-    load_win.start()
-
-    small = [
-        pltpu.make_async_copy(source, target, local_sem.at[4 + k])
-        for k, (source, target) in enumerate(
-            (
-                (owner_h, owner),
-                (table_h, table),
-                (length_h, length),
-                (gain_h, gain),
-                (lq1_h, lq1),
-                (lk1_h, lk1),
-                (lq2_h, lq2),
-                (lk2_h, lk2),
-            )
-        )
-    ]
-    for load in small:
-        load.start()
     pl.semaphore_wait(barrier, 3 + len(x_near) + len(z_near))
 
     quarter = count // 4
@@ -310,6 +288,28 @@
 
     started = gather_start(x, tokens, x_send, x_recv)
     greet(0)
+    local_x = pltpu.make_async_copy(tokens, x.at[me_h], local_sem.at[0])
+    local_x.start()
+    load_win = pltpu.make_async_copy(w_in, win_v, local_sem.at[1])
+    load_win.start()
+
+    small = [
+        pltpu.make_async_copy(source, target, local_sem.at[4 + k])
+        for k, (source, target) in enumerate(
+            (
+                (owner_h, owner),
+                (table_h, table),
+                (length_h, length),
+                (gain_h, gain),
+                (lq1_h, lq1),
+                (lk1_h, lk1),
+                (lq2_h, lq2),
+                (lk2_h, lk2),
+            )
+        )
+    ]
+    for load in small:
+        load.start()
 
     def prepare():
         for load in small:
@@ -430,12 +430,11 @@
         cut = slice(h * half, (h + 1) * half)
         at = info[0:1, cut]
         for ref, lo in ((first_a, 0), (first_b, QK)):
-            kept = None
-            for p in range(0, SHARED, 2):
-                keys = pool_v[p : p + 2].reshape(2 * PAGE, WIDE)[:, lo : lo + QK]
-                score = dot_nt(keys, queries[cut, lo : lo + QK])
-                chosen = jnp.where(at == float(p), score[0:PAGE], score[PAGE:])
-                kept = chosen if p == 0 else jnp.where(at >= float(p), chosen, kept)
+            keys = pool_v[0:SHARED].reshape(SHARED * PAGE, WIDE)[:, lo : lo + QK]
+            score = dot_nt(keys, queries[cut, lo : lo + QK])
+            kept = score[0:PAGE]
+            for p in range(1, SHARED):
+                kept = jnp.where(at == float(p), score[p * PAGE : (p + 1) * PAGE], kept)
             ref[:, cut] = kept
 
     row = iota((2 * GROUP, LANES), 0) % GROUP

time: 42 us -> 41.8 us (level)
  no operation moved by 1% of the time
where the time goes in v7:
time: 41.8 us; the launch traced here: 41.7 us
  Pallas kernels  41 us (98%)
  local copies, waits for them, and re-layouts  0.66 us (2%)
    pallas_call x1, Pallas kernels, on_device(): pl.pallas_call(functools.partial(step_kernel, sizes), out_shape=pltpu.VME...  41 us

profile of v7, /device:TPU:1, one launch (start us, length us, event | category | flops | bytes accessed | tf_op | source)
XLA Modules:
  0.0 41.7 jit_solution(244528471378386101)
XLA Ops:
  0.0 41.0 %decode_step.1 = bf16[256,256]{1,0:T(8,128)(2,1)S(1)} custom-call(bf16[256,256]{1,0:T(8,128)(2,1)} %tokens.1, bf16[2048,768]{1,0:T(8,128)(2,1)} %w_in.1, bf16[256,2048]{1,0:T(8,128)(2,1)} %w_out.1, bf16[64,128,512]{2,1,0:T(8,128)(2,1)} %bitcast.9, f32[1,256]{1,0:T(1,128)} %bitcast.11, f32[1,128]{1,0:T(1,128)} %bitcast.14, f32[1,128]{1,0:T(1,128)} %bitcast.15, ...), custom_call_target="tpu_custom_call" | custom-call | tf_op jit(solution)/shard_map/decode_step/pallas_call | solution.py:557
  41.0 0.7 %copy.14 = bf16[256,256]{1,0:T(8,128)(2,1)} copy(bf16[256,256]{1,0:T(8,128)(2,1)S(1)} %decode_step.1) | data formatting | bytes 262144

commit v8 on v7

--- a/solution.py
+++ b/solution.py
@@ -238,11 +238,14 @@
 
     def gather_rest(started, add, beside):
         go, copies = started
+        crossed = []
         for k, (source, start, target) in enumerate(
             ((h_down, 0, h_up), (h_up, 3, h_down), (h_down, 1, h_up), (h_up, 2, h_down))
         ):
             copies[k].wait_recv()
             copies.append(go(7 + k, source, start, 1, target))
+            if k >= 2:
+                crossed.append(go(15 + k, source, start, 1, (a_up, a_down)[k - 2]))
         copies.append(go(11, h_down, 0, 2, sib))
         copies.append(go(12, h_up, 2, 2, sib))
         beside(1)
@@ -262,13 +265,15 @@
         copies[12].wait_recv()
         copies[14].wait_recv()
         add(a_up)
-        for k, start in enumerate((0, 3, 1, 2)):
+        for k, start in enumerate((0, 3)):
             copies[7 + k].wait_recv()
             copies.append(go(15 + k, h_far, start, 1, sib))
         beside(3)
+        copies[9].wait_recv()
+        copies[10].wait_recv()
         add(h_far)
-        for k in range(4):
-            copies[15 + k].wait_recv()
+        for copy in copies[15:] + crossed:
+            copy.wait_recv()
         add(a_far)
 
     def tiles(rows, height, target):

time: 41.8 us -> 40.8 us (0.976)
  Pallas kernels: 41 us -> 40 us
    pallas_call x1, Pallas kernels: 41 us -> 40 us  [on_device(): pl.pallas_call(functools.partial(step_kernel, sizes), out_shape=pltpu.VME...]
where the time goes in v8:
time: 40.8 us; the launch traced here: 40.7 us
  Pallas kernels  40 us (98%)
  local copies, waits for them, and re-layouts  0.66 us (2%)
    pallas_call x1, Pallas kernels, on_device(): pl.pallas_call(functools.partial(step_kernel, sizes), out_shape=pltpu.VME...  40 us

profile of v8, /device:TPU:1, one launch (start us, length us, event | category | flops | bytes accessed | tf_op | source)
XLA Modules:
  0.0 40.7 jit_solution(11472041048330916229)
XLA Ops:
  0.0 40.0 %decode_step.1 = bf16[256,256]{1,0:T(8,128)(2,1)S(1)} custom-call(bf16[256,256]{1,0:T(8,128)(2,1)} %tokens.1, bf16[2048,768]{1,0:T(8,128)(2,1)} %w_in.1, bf16[256,2048]{1,0:T(8,128)(2,1)} %w_out.1, bf16[64,128,512]{2,1,0:T(8,128)(2,1)} %bitcast.9, f32[1,256]{1,0:T(1,128)} %bitcast.11, f32[1,128]{1,0:T(1,128)} %bitcast.14, f32[1,128]{1,0:T(1,128)} %bitcast.15, ...), custom_call_target="tpu_custom_call" | custom-call | tf_op jit(solution)/shard_map/decode_step/pallas_call | solution.py:562
  40.0 0.7 %copy.14 = bf16[256,256]{1,0:T(8,128)(2,1)} copy(bf16[256,256]{1,0:T(8,128)(2,1)S(1)} %decode_step.1) | data formatting | bytes 262144
